TPU v7x, 32 devices: a whole 2x2x4 slice. The times are simulated.
32 devices in a mesh: dp: 2 (over x), slab: 16 (over z, y, core).
Axes of the slice: x: 2, y: 2, z: 4, core: 2. Of those that a mesh axis runs over, the one named last changes fastest.
Arguments:
- images: float32 [512, 128, 128], P(('dp', 'slab')), may hold values from -6 to 6
- defocus: float32 [512], P(('dp', 'slab')), may hold values from 8 to 40
- references: float32 [512, 64, 128], P('slab'), may hold values from -6 to 6
- orient_owner: int32 [512, 4], P(('dp', 'slab')), may hold values from 0 to 15, all different within a row; in each aligned block of 16 rows (0 to 15, 16 to 31, ...) at most 8 rows name the same one
- orient_local: int32 [512, 4], P(('dp', 'slab')), may hold values from 0 to 31
- block_owner: int32 [512, 8, 1], P('slab'), may hold values from 0 to 15; in each aligned block of 256 rows (0 to 255, 256 to 511, ..., all dimensions but the last counted through in order) at most 32 rows name the same one
- block_cell: int32 [512, 8], P('slab'), may hold values from 0 to 511
Outputs:
- posterior: float32 [512, 4], P(('dp', 'slab'))
- volume: float32 [64, 256, 2, 256], P('slab', 'dp')
Inputs may be any that keep to these rules, and one draw needn't show every extreme that they name: `orient_owner`: within the 16 particles of one device (aligned blocks of rows), no slab index is named by more than 8 entries, and some slab index is named by exactly 8; the 4 entries of a particle differ. `block_owner`: within the 256 blocks of one slab index's references (aligned blocks of rows), no slab index is named by more than 32 entries, and some slab index is named by exactly 32.
All inputs are finite; a program needn't handle non-finite values.
Results may differ from a plain program's by a relative error of at most 0.00015.
Values sent between devices are 32-bit elements; how exact they have to be, the bound alone decides.
A program may use at most 64 MiB of HBM per device.

v0:
```python
import math

import jax
import jax.numpy as jnp
from jax import lax
from jax.sharding import PartitionSpec as P

VY = 256
VX = 256
ZDEV = 4


HIGH_PRECISION = lax.Precision.HIGHEST
AMPLITUDE = 0.1
EPSILON = 1e-05


def freq_tables(image_side, frequency_total):
    pixels = jnp.arange(image_side, dtype=jnp.int32)
    freqs = jnp.arange(frequency_total, dtype=jnp.int32) - frequency_total // 2
    phase = jnp.mod(pixels[:, None] * freqs[None, :], image_side).astype(jnp.float32) * (
        2.0 * math.pi / image_side
    )
    return (jnp.cos(phase), jnp.sin(phase))


def contrast(defocus, frequency_total):
    freqs = (jnp.arange(frequency_total, dtype=jnp.int32) - frequency_total // 2).astype(
        jnp.float32
    )
    radius = (freqs[:, None] * freqs[:, None] + freqs[None, :] * freqs[None, :]) / float(
        (frequency_total // 2) ** 2
    )
    phase = defocus[:, None, None] * radius[None]
    return -(math.sqrt(1.0 - AMPLITUDE * AMPLITUDE) * jnp.sin(phase) + AMPLITUDE * jnp.cos(phase))


def spectra_of(images, defocus, frequency_total):
    image_side = images.shape[-1]
    cosine, sine = freq_tables(image_side, frequency_total)
    first_pass = jnp.einsum(
        "pyx,xf->pyf", images, jnp.concatenate([cosine, -sine], axis=1), precision=HIGH_PRECISION
    )
    lower_half = jnp.concatenate(
        [first_pass[..., frequency_total:], -first_pass[..., :frequency_total]], axis=2
    )
    spectra = jnp.einsum("yf,pyg->pfg", cosine, first_pass, precision=HIGH_PRECISION) + jnp.einsum(
        "yf,pyg->pfg", sine, lower_half, precision=HIGH_PRECISION
    )
    factor = contrast(defocus, frequency_total) / image_side
    return spectra * jnp.concatenate([factor, factor], axis=2)


def score_slots(chosen, received, image_side):
    frequency_total = received.shape[1]
    cosine, sine = freq_tables(image_side, frequency_total)
    rotation_angle = jnp.concatenate(
        [jnp.concatenate([cosine.T, sine.T], axis=1), jnp.concatenate([-sine.T, cosine.T], axis=1)],
        axis=0,
    )
    inverted_rows = jnp.concatenate([cosine, -sine], axis=1)
    slot_total = received.shape[0]
    group_size = math.gcd(slot_total, 16)

    def one_group(couple):
        ref_part, spec_part = couple
        ref_re, ref_im = (ref_part[..., :frequency_total], ref_part[..., frequency_total:])
        spec_re, spec_im = (spec_part[..., :frequency_total], spec_part[..., frequency_total:])
        spectral_product = jnp.concatenate(
            [ref_re * spec_re + ref_im * spec_im, ref_re * spec_im - ref_im * spec_re], axis=2
        )
        center_index = jnp.einsum(
            "eio,ol->eil", spectral_product, rotation_angle, precision=HIGH_PRECISION
        )
        stacked_planes = jnp.concatenate(
            [center_index[..., :image_side], center_index[..., image_side:]], axis=1
        )
        translation_offsets = (
            jnp.einsum("kz,wzq->wkq", inverted_rows, stacked_planes, precision=HIGH_PRECISION)
            / frequency_total
        )
        return (
            jnp.max(
                (translation_offsets * translation_offsets).reshape(
                    translation_offsets.shape[0], -1
                ),
                axis=1,
            )
            + EPSILON
        )

    grouped = (
        chosen.reshape((slot_total // group_size, group_size) + chosen.shape[1:]),
        received.reshape((slot_total // group_size, group_size) + received.shape[1:]),
    )
    return lax.map(one_group, grouped).reshape(-1)


def slot_ranks(owner_ids, owner_count):
    owner_hits = (owner_ids[:, None] == jnp.arange(owner_count, dtype=jnp.int32)[None, :]).astype(
        jnp.int32
    )
    return jnp.sum((jnp.cumsum(owner_hits, axis=0) - 1) * owner_hits, axis=1)


def insert(blocks, cell_ids, planes, row_blocks, col_blocks, first_block, span_blocks):
    band_rows, row_width = (blocks.shape[2], blocks.shape[3])
    frequency_total = row_width // 2
    flat_rows = blocks.reshape(-1, band_rows * row_width)
    cell_ids = cell_ids.reshape(-1)
    plane_of = cell_ids // (row_blocks * col_blocks)
    row_of = cell_ids // col_blocks % row_blocks - first_block
    column_of = cell_ids % col_blocks
    usable = (cell_ids >= 0) & (row_of >= 0) & (row_of < span_blocks)
    target = jnp.where(usable, (plane_of * span_blocks + row_of) * col_blocks + column_of, -1)
    placing = (
        jnp.arange(planes * span_blocks * col_blocks, dtype=jnp.int32)[:, None] == target[None, :]
    ).astype(jnp.float32)
    placed = jnp.dot(placing, flat_rows, precision=HIGH_PRECISION)
    placed = placed.reshape(planes, span_blocks, col_blocks, band_rows, 2, frequency_total)
    return placed.transpose(0, 1, 3, 4, 2, 5).reshape(
        planes, span_blocks * band_rows, 2, col_blocks * frequency_total
    )


def per_device(images, defocus, references, orient_owner, orient_local, block_owner, block_cell):
    owner_count = lax.axis_size("slab")
    frequency_total = references.shape[1]
    image_side = images.shape[-1]
    part_count, pick_count = orient_owner.shape
    ref_rows = references.shape[0]
    slot_cap = max(2, 2 * part_count * pick_count // owner_count)
    spectra = spectra_of(images, defocus, frequency_total)
    flat_owner = orient_owner.reshape(-1)
    slot_of = flat_owner * slot_cap + slot_ranks(flat_owner, owner_count)
    particle_of = jnp.arange(part_count * pick_count, dtype=jnp.int32) // pick_count
    send_spectra = jnp.zeros(
        (owner_count * slot_cap, frequency_total, 2 * frequency_total), jnp.float32
    )
    send_spectra = send_spectra.at[slot_of].set(jnp.repeat(spectra, pick_count, axis=0))
    send_meta = jnp.full((owner_count * slot_cap, 2), -1, jnp.int32)
    send_meta = send_meta.at[slot_of].set(
        jnp.stack([orient_local.reshape(-1), particle_of], axis=1)
    )
    received, meta_in = (
        lax.all_to_all(
            send_spectra.reshape(owner_count, slot_cap, frequency_total, 2 * frequency_total),
            "slab",
            split_axis=0,
            concat_axis=0,
            tiled=True,
        ),
        lax.all_to_all(
            send_meta.reshape(owner_count, slot_cap, 2),
            "slab",
            split_axis=0,
            concat_axis=0,
            tiled=True,
        ),
    )
    flat_received = received.reshape(-1, frequency_total, 2 * frequency_total)
    ref_index = meta_in[..., 0].reshape(-1)
    chosen = references[jnp.clip(ref_index, 0, ref_rows - 1)]
    scores = score_slots(chosen, flat_received, image_side)
    slot_scores = scores.reshape(owner_count, slot_cap)
    back_scores = lax.all_to_all(slot_scores, "slab", split_axis=0, concat_axis=0, tiled=True)
    item_scores = back_scores.reshape(-1)[slot_of].reshape(part_count, pick_count)
    posterior = item_scores / jnp.sum(item_scores, axis=1, keepdims=True)
    slot_weight = (
        jnp.zeros((owner_count * slot_cap,), jnp.float32).at[slot_of].set(posterior.reshape(-1))
    )
    got_weight = lax.all_to_all(
        slot_weight.reshape(owner_count, slot_cap), "slab", split_axis=0, concat_axis=0, tiled=True
    ).reshape(-1)
    ref_hits = (ref_index[None, :] == jnp.arange(ref_rows, dtype=jnp.int32)[:, None]).astype(
        jnp.float32
    ) * got_weight[None, :]
    averages = jnp.dot(
        ref_hits, flat_received.reshape(flat_received.shape[0], -1), precision=HIGH_PRECISION
    )
    averages = averages.reshape(ref_rows, frequency_total, 2 * frequency_total)
    bands = block_cell.shape[1]
    band_rows = frequency_total // bands
    block_cap = max(2, 2 * ref_rows * bands // owner_count)
    dest_owner = block_owner.reshape(-1)
    block_slot = dest_owner * block_cap + slot_ranks(dest_owner, owner_count)
    cell_send = (
        jnp.full((owner_count * block_cap,), -1, jnp.int32)
        .at[block_slot]
        .set(block_cell.reshape(-1))
    )
    row_blocks = VY // band_rows
    col_blocks = VX // frequency_total
    pieces = averages.reshape(ref_rows * bands, band_rows, 2 * frequency_total)
    block_send = (
        jnp.zeros((owner_count * block_cap, band_rows, 2 * frequency_total), jnp.float32)
        .at[block_slot]
        .set(pieces)
    )
    blocks_in = lax.all_to_all(
        block_send.reshape(owner_count, block_cap, band_rows, 2 * frequency_total),
        "slab",
        split_axis=0,
        concat_axis=0,
        tiled=True,
    )
    cells_in = lax.all_to_all(
        cell_send.reshape(owner_count, block_cap), "slab", split_axis=0, concat_axis=0, tiled=True
    )
    partial_value = insert(blocks_in, cells_in, ZDEV, row_blocks, col_blocks, 0, row_blocks)
    volume = lax.psum_scatter(partial_value, "dp", scatter_dimension=1, tiled=True)
    return (posterior, volume)


def solution(mesh):
    in_specs = (
        P(("dp", "slab"), None, None),
        P(("dp", "slab")),
        P("slab", None, None),
        P(("dp", "slab"), None),
        P(("dp", "slab"), None),
        P("slab", None, None),
        P("slab", None),
    )
    out_specs = (P(("dp", "slab"), None), P("slab", "dp", None, None))
    return jax.shard_map(
        per_device, mesh=mesh, in_specs=in_specs, out_specs=out_specs, check_vma=False
    )
```

profile of v0, /device:TPU:0, one launch (start us, length us, event | category | flops | bytes accessed | tf_op | source)
XLA Modules:
  0.0 349.9 jit_solution(11462684940681356369)
XLA Ops:
  11.9 7.4 %all-to-all-start = ((s32[16,8,2]{1,2,0:T(2,128)}), s32[16,8,2]{1,2,0:T(2,128)S(1)}, u32[]{:S(2)}, u32[]{:S(2)}) async-start(s32[16,8,2]{1,2,0:T(2,128)} %copy.41), calls=%async_computation | async-start | bytes 32768 | tf_op jit(solution)/shard_map/all_to_all | solution.py:153
  19.5 2.2 convolution_bitcast_fusion.1
  23.4 2.0 fusion.26
  27.1 2.5 broadcast_in_dim.18
  29.6 8.6 %scatter_fusion = f32[128,64,128]{2,1,0:T(8,128)} fusion(f32[128,64,128]{2,1,0:T(8,128)} %broadcast_in_dim.18, s32[64]{0:T(128)S(1)} %fusion.74, f32[64,64,128]{2,1,0:T(8,128)S(1)} %bitcast.106), kind=kCustom, calls=%fused_computation.3 | custom fusion | bytes 6291712 | tf_op jit(solution)/shard_map/scatter | solution.py:140
  38.2 6.2 %all-to-all-start.1 = ((f32[16,8,64,128]{3,2,1,0:T(8,128)}), f32[16,8,64,128]{3,2,1,0:T(8,128)}, u32[]{:S(2)}, u32[]{:S(2)}) async-start(f32[16,8,64,128]{3,2,1,0:T(8,128)} %bitcast.104), calls=%async_computation.1 | async-start | bytes 8388608 | tf_op jit(solution)/shard_map/all_to_all | solution.py:146
  46.1 2.8 gather_fusion
  48.9 73.1 %all-to-all-done.1 = f32[16,8,64,128]{3,2,1,0:T(8,128)} async-done(((f32[16,8,64,128]{3,2,1,0:T(8,128)}), f32[16,8,64,128]{3,2,1,0:T(8,128)}, u32[]{:S(2)}, u32[]{:S(2)}) %all-to-all-start.1) | async-done | bytes 4194336 | tf_op jit(solution)/shard_map/all_to_all | solution.py:146
  122.1 37.9 %while.10 = (s32[]{:T(128)}, f32[8,16]{1,0:T(8,128)S(1)}, f32[8,16,64,128]{3,2,1,0:T(8,128)}, f32[8,16,64,128]{3,2,1,0:T(8,128)}, f32[128,256]{1,0:T(8,128)S(1)}...) while((s32[]{:T(128)}, f32[8,16]{1,0:T(8,128)S(1)}, f32[8,16,64,128]{3,2,1,0:T(8,128)}, ...), condition=%wide.region_6.7_spmd, body=%wide.region_4.6_spmd.sunk | while | flops 806879232 | bytes 8585629 | solution.py:96
  124.9 1.9 fusion.106
  129.6 1.9 fusion.106
  134.4 1.9 fusion.106
  139.1 1.9 fusion.106
  143.8 1.9 fusion.106
  148.6 1.9 fusion.106
  153.3 1.9 fusion.106
  158.1 1.9 fusion.106
  160.7 19.6 %all-to-all-start.2 = ((f32[16,1,8]{2,1,0:T(1,128)}), f32[16,1,8]{2,1,0:T(1,128)S(1)}, u32[]{:S(2)}, u32[]{:S(2)}) async-start(f32[16,1,8]{2,1,0:T(1,128)} %bitcast.18), calls=%async_computation.2 | async-start | bytes 16384 | tf_op jit(solution)/shard_map/all_to_all | solution.py:166
  180.5 6.2 %all-to-all-done.2 = f32[16,1,8]{2,1,0:T(1,128)S(1)} async-done(((f32[16,1,8]{2,1,0:T(1,128)}), f32[16,1,8]{2,1,0:T(1,128)S(1)}, u32[]{:S(2)}, u32[]{:S(2)}) %all-to-all-start.2) | async-done | bytes 544 | tf_op jit(solution)/shard_map/all_to_all | solution.py:166
  190.6 3.5 all-to-all-start.4
  196.4 3.9 %all-to-all-done.4 = f32[16,1,8]{2,1,0:T(1,128)S(1)} async-done(((f32[16,1,8]{2,1,0:T(1,128)}), f32[16,1,8]{2,1,0:T(1,128)S(1)}, u32[]{:S(2)}, u32[]{:S(2)}) %all-to-all-start.4) | async-done | bytes 544 | tf_op jit(solution)/shard_map/all_to_all | solution.py:172
  200.4 3.4 all-to-all-start.3
  204.6 7.0 %fusion.13 = f32[32,8192]{1,0:T(8,128)S(1)} fusion(f32[16,8,64,128]{3,2,1,0:T(8,128)} %all-to-all-done.1, f32[128]{0:T(128)S(1)} %mul.232, s32[128]{0:T(128)S(1)} %eq.112), kind=kOutput, calls=%fused_computation.26 | convolution fusion | flops 402661376 | bytes 5243904 | tf_op jit(solution)/shard_map/dot_general | solution.py:178
  213.2 23.9 %scatter_fusion.1 = f32[512,8,128]{2,1,0:T(8,128)} fusion(f32[512,8,128]{2,1,0:T(8,128)} %broadcast_in_dim.21, s32[256]{0:T(256)S(1)} %bitcast.112, f32[256,8,128]{2,1,0:T(8,128)S(1)} %reshape.415), kind=kCustom, calls=%fused_computation.6 | custom fusion | bytes 3146752 | tf_op jit(solution)/shard_map/scatter | solution.py:198
  237.1 6.0 %all-to-all-start.5 = ((f32[16,32,8,128]{3,2,1,0:T(8,128)}), f32[16,32,8,128]{3,2,1,0:T(8,128)S(1)}, u32[]{:S(2)}, u32[]{:S(2)}) async-start(f32[16,32,8,128]{3,2,1,0:T(8,128)} %bitcast.25), calls=%async_computation.5 | async-start | bytes 4194304 | tf_op jit(solution)/shard_map/all_to_all | solution.py:200
  244.5 39.8 %all-to-all-done.5 = f32[16,32,8,128]{3,2,1,0:T(8,128)S(1)} async-done(((f32[16,32,8,128]{3,2,1,0:T(8,128)}), f32[16,32,8,128]{3,2,1,0:T(8,128)S(1)}, u32[]{:S(2)}, u32[]{:S(2)}) %all-to-all-start.5) | async-done | bytes 2097184 | tf_op jit(solution)/shard_map/all_to_all | solution.py:200
  286.1 1.9 copy.52
  288.0 3.6 %convolution_bitcast_fusion = f32[4,32,8,2,4,64]{5,1,3,2,4,0:T(8,128)S(1)} fusion(f32[8,2,64,512,1,1]{3,2,1,0,5,4:T(8,128)S(1)} %bitcast.107, s32[512]{0:T(512)S(1)} %fusion.70, s32[4,32,4]{1,2,0:T(4,128)S(1)} %multiply_add_fusion.1), kind=kOutput, calls=%fused_computation.29 | convolution fusion | flops 3221487616 | bytes 4198400 | tf_op jit(solution)/shard_map/dot_general | solution.py:119
  291.6 4.6 %copy.53 = f32[4,32,8,2,4,64]{5,4,2,1,3,0:T(4,128)} copy(f32[4,32,8,2,4,64]{5,1,3,2,4,0:T(8,128)S(1)} %convolution_bitcast_fusion) | data formatting | bytes 4194304 | tf_op jit(solution)/shard_map/transpose | solution.py:121
  296.2 5.3 %reshape.362 = f32[4,256,2,256]{3,1,2,0:T(8,128)} reshape(f32[4,32,8,2,4,64]{5,4,2,1,3,0:T(4,128)} %copy.53) | data formatting | bytes 4194304 | tf_op jit(solution)/shard_map/reshape | solution.py:121
  302.3 37.8 %reduce-scatter.2.cloned.1.call-done = f32[4,128,2,256]{3,1,2,0:T(8,128)} async-done(((f32[4,256,2,256]{3,1,2,0:T(8,128)}), f32[4,128,2,256]{3,1,2,0:T(8,128)}) %reduce-scatter.2.cloned.1.call-update) | async-done | bytes 1048592 | tf_op jit(solution)/shard_map/reduce_scatter | solution.py:211
  340.1 3.0 copy.55
  (136 shorter events, 45.6 us)
Async XLA Ops:
  7.2 39.0 %copy-start = (f32[32,64,128]{2,1,0:T(8,128)S(1)}, f32[32,64,128]{2,1,0:T(8,128)}, u32[]{:S(2)}) copy-start(f32[32,64,128]{2,1,0:T(8,128)} %param.11) | copy-start | bytes 3145732
  7.2 16.2 %copy-start.3 = (f32[16]{0:T(128)S(1)}, f32[16]{0:T(128)}, u32[]{:S(2)}) copy-start(f32[16]{0:T(128)} %param.10) | copy-start | bytes 196
  11.9 26.4 %all-to-all-start = ((s32[16,8,2]{1,2,0:T(2,128)}), s32[16,8,2]{1,2,0:T(2,128)S(1)}, u32[]{:S(2)}, u32[]{:S(2)}) async-start(s32[16,8,2]{1,2,0:T(2,128)} %copy.41), calls=%async_computation | async-start | bytes 32768 | tf_op jit(solution)/shard_map/all_to_all | solution.py:153
  38.2 6.2 %copy-start.1 = (s32[32,8,1]{0,2,1:T(1,128)S(1)}, s32[32,8,1]{0,2,1:T(1,128)}, u32[]{:S(2)}) copy-start(s32[32,8,1]{0,2,1:T(1,128)} %param.14) | copy-start | bytes 3076
  38.2 83.8 %all-to-all-start.1 = ((f32[16,8,64,128]{3,2,1,0:T(8,128)}), f32[16,8,64,128]{3,2,1,0:T(8,128)}, u32[]{:S(2)}, u32[]{:S(2)}) async-start(f32[16,8,64,128]{3,2,1,0:T(8,128)} %bitcast.104), calls=%async_computation.1 | async-start | bytes 8388608 | tf_op jit(solution)/shard_map/all_to_all | solution.py:146
  122.1 72.0 %copy-start.2 = (s32[32,8]{0,1:T(8,128)S(1)}, s32[32,8]{0,1:T(8,128)}, u32[]{:S(2)}) copy-start(s32[32,8]{0,1:T(8,128)} %param.15) | copy-start | bytes 3076
  160.7 26.0 %all-to-all-start.2 = ((f32[16,1,8]{2,1,0:T(1,128)}), f32[16,1,8]{2,1,0:T(1,128)S(1)}, u32[]{:S(2)}, u32[]{:S(2)}) async-start(f32[16,1,8]{2,1,0:T(1,128)} %bitcast.18), calls=%async_computation.2 | async-start | bytes 16384 | tf_op jit(solution)/shard_map/all_to_all | solution.py:166
  190.6 9.8 %all-to-all-start.4 = ((f32[16,1,8]{2,1,0:T(1,128)}), f32[16,1,8]{2,1,0:T(1,128)S(1)}, u32[]{:S(2)}, u32[]{:S(2)}) async-start(f32[16,1,8]{2,1,0:T(1,128)} %bitcast.24), calls=%async_computation.4 | async-start | bytes 16384 | tf_op jit(solution)/shard_map/all_to_all | solution.py:172
  200.4 36.7 %all-to-all-start.3 = ((s32[16,1,32]{2,1,0:T(1,128)}), s32[16,1,32]{2,1,0:T(1,128)S(1)}, u32[]{:S(2)}, u32[]{:S(2)}) async-start(s32[16,1,32]{2,1,0:T(1,128)} %all_to_all.31), calls=%async_computation.3 | async-start | bytes 16384 | tf_op jit(solution)/shard_map/all_to_all | solution.py:207
  237.1 47.1 %all-to-all-start.5 = ((f32[16,32,8,128]{3,2,1,0:T(8,128)}), f32[16,32,8,128]{3,2,1,0:T(8,128)S(1)}, u32[]{:S(2)}, u32[]{:S(2)}) async-start(f32[16,32,8,128]{3,2,1,0:T(8,128)} %bitcast.25), calls=%async_computation.5 | async-start | bytes 4194304 | tf_op jit(solution)/shard_map/all_to_all | solution.py:200
  243.1 96.9 %reduce-scatter.2.cloned.1.call-start = ((), (), s32[]{:S(2)}) async-start(), calls=%async_computation.7 | async-start | bytes 3145728 | tf_op jit(solution)/shard_map/reduce_scatter | solution.py:211
Sparse Core Ops, SparseCore 0:
  301.7 38.3 reduce-scatter.1
where the time goes:
time: 352 us; the launch traced here: 350 us
  waiting for transfers between devices  161 us (46%)
  local copies, waits for them, and re-layouts  79.6 us (23%)
  starting transfers between devices  46.1 us (13%)
  matrix products  39.3 us (11%)
  between operations  14.4 us (4%)
  other arithmetic  9.44 us (3%)
    all_to_all x1, waiting for transfers between devices, per_device(): lax.all_to_all(send_spectra.reshape(owner_count, slot_cap, frequency_tota...  73.1 us
    all_to_all x1, waiting for transfers between devices, per_device(): lax.all_to_all(block_send.reshape(owner_count, block_cap, band_rows, 2 *...  39.8 us
    reduce_scatter x1, waiting for transfers between devices, per_device(): lax.psum_scatter(partial_value, 'dp', scatter_dimension=1, tiled=True)  37.8 us
    scatter x1, local copies, waits for them, and re-layouts, per_device(): block_send = jnp.zeros((owner_count * block_cap, band_rows, 2 * frequency...  23.9 us
    all_to_all x1, starting transfers between devices, per_device(): lax.all_to_all(slot_scores, 'slab', split_axis=0, concat_axis=0, tiled=True)  19.6 us
    dot_general x8, matrix products, one_group(): jnp.einsum('kz,wzq->wkq', inverted_rows, stacked_planes, precision=HIGH_P...  15.3 us
    squeeze x8, local copies, waits for them, and re-layouts, score_slots(): return lax.map(one_group, grouped).reshape(-1)  10.2 us
    scatter x1, local copies, waits for them, and re-layouts, per_device(): send_spectra.at[slot_of].set(jnp.repeat(spectra, pick_count, axis=0))  8.65 us
  transfers between devices with their start and end apart: 7, of which 5 were waited for; matrix products, arithmetic and copies ran while one was open for 17% of the time, Pallas kernels for 0%

commit v1 on v0

--- a/solution.py
+++ b/solution.py
@@ -1,8 +1,12 @@
+import functools
 import math
 
 import jax
 import jax.numpy as jnp
+import numpy as np
 from jax import lax
+from jax.experimental import pallas as pl
+from jax.experimental.pallas import tpu as pltpu
 from jax.sharding import PartitionSpec as P
 
 VY = 256
@@ -212,6 +216,358 @@
     return (posterior, volume)
 
 
+HALF_PRECISION = lax.Precision.HIGH
+MESH = pl.DeviceIdType.MESH
+
+
+def ring_place(pos, depth):
+    back = pos // depth
+    z = (1 - back) * pos + back * (2 * depth - 1 - pos)
+    return z * 2 + back
+
+
+def gather_kernel(chips, own_ref, out_ref, local_sem, ring_send, ring_recv, pair_send, pair_recv):
+    depth = chips // 2
+    me = lax.axis_index("slab")
+    core = me % 2
+    chip = me // 2
+    z, back = chip // 2, chip % 2
+    pos = z + back * (2 * depth - 1 - 2 * z)
+    dirs = ((pos + 1) % chips, (pos + chips - 1) % chips)
+    targets = [ring_place(q, depth) * 2 + core for q in dirs]
+    sibling = chip * 2 + 1 - core
+    barrier = pltpu.get_barrier_semaphore()
+    for other in targets + [sibling]:
+        pl.semaphore_signal(barrier, inc=1, device_id={"slab": other}, device_id_type=MESH)
+    pl.semaphore_wait(barrier, 3)
+    part = own_ref.shape[0] // 2
+    rows = lambda ref, h: ref.at[pl.ds(h * part, part)]
+    local = pltpu.make_async_copy(own_ref, out_ref.at[me], local_sem)
+    local.start()
+    waits = []
+
+    def ring_copy(src, origin, d, t, h):
+        return pltpu.make_async_remote_copy(
+            src_ref=src, dst_ref=rows(out_ref.at[origin], h),
+            send_sem=ring_send.at[d, t, h], recv_sem=ring_recv.at[d, t, h],
+            device_id={"slab": targets[d]}, device_id_type=MESH)
+
+    def pair_copy(src, origin, n, h):
+        return pltpu.make_async_remote_copy(
+            src_ref=src, dst_ref=rows(out_ref.at[origin], h),
+            send_sem=pair_send.at[n, h], recv_sem=pair_recv.at[n, h],
+            device_id={"slab": sibling}, device_id_type=MESH)
+
+    def origin_of(d, t):
+        q = (pos + chips - t) % chips if d == 0 else (pos + t) % chips
+        return ring_place(q, depth) * 2 + core
+
+    hops = [(d, t, h) for t in range(depth) for h in range(2) for d in range(2)
+            if t < depth - 1 or h == d]
+    pair_of = lambda d, t, h: (t + 1 if d == 0 else depth + t + 1) if t < depth - 1 else depth
+    for d, t, h in hops:
+        if t == 0:
+            copy = ring_copy(rows(own_ref, h), me, d, 0, h)
+            copy.start()
+            waits.append(copy)
+    for h in range(2):
+        copy = pair_copy(rows(own_ref, h), me, 0, h)
+        copy.start()
+        waits.append(copy)
+    pairs = []
+    for d, t, h in hops:
+        origin = origin_of(d, t + 1)
+        landed = rows(out_ref.at[origin], h)
+        ring_copy(landed, origin, d, t, h).wait_recv()
+        if (d, t + 1, h) in hops:
+            copy = ring_copy(landed, origin, d, t + 1, h)
+            copy.start()
+            waits.append(copy)
+        copy = pair_copy(landed, origin, pair_of(d, t, h), h)
+        copy.start()
+        pairs.append(copy)
+        waits.append(copy)
+    for copy in waits:
+        copy.wait_send()
+    pair_copy(rows(own_ref, 0), me, 0, 0).wait_recv()
+    pair_copy(rows(own_ref, 1), me, 0, 1).wait_recv()
+    for copy in pairs:
+        copy.wait_recv()
+    local.wait()
+
+
+def ring_gather(payload, owner_count):
+    chips = owner_count // 2
+    depth = chips // 2
+    return pl.pallas_call(
+        functools.partial(gather_kernel, chips),
+        out_shape=jax.ShapeDtypeStruct((owner_count,) + payload.shape, payload.dtype),
+        in_specs=[pl.BlockSpec(memory_space=pl.ANY)],
+        out_specs=pl.BlockSpec(memory_space=pl.ANY),
+        scratch_shapes=[
+            pltpu.SemaphoreType.DMA,
+            pltpu.SemaphoreType.DMA((2, depth, 2)),
+            pltpu.SemaphoreType.DMA((2, depth, 2)),
+            pltpu.SemaphoreType.DMA((chips, 2)),
+            pltpu.SemaphoreType.DMA((chips, 2)),
+        ],
+        compiler_params=pltpu.CompilerParams(collective_id=1, has_side_effects=True),
+        name="ring_gather",
+    )(payload)
+
+
+def share_kernel(count, own_ref, out_ref, local_sem, send_sem, recv_sem):
+    me = lax.axis_index("slab")
+    barrier = pltpu.get_barrier_semaphore()
+    others = [(me + step) % count for step in range(1, count)]
+    for other in others:
+        pl.semaphore_signal(barrier, inc=1, device_id={"slab": other}, device_id_type=MESH)
+    local = pltpu.make_async_copy(own_ref, out_ref.at[me], local_sem)
+    local.start()
+    pl.semaphore_wait(barrier, count - 1)
+    copies = []
+    for n, other in enumerate(others):
+        copy = pltpu.make_async_remote_copy(
+            src_ref=own_ref, dst_ref=out_ref.at[me], send_sem=send_sem.at[n],
+            recv_sem=recv_sem.at[n], device_id={"slab": other}, device_id_type=MESH)
+        copy.start()
+        copies.append(copy)
+    for n, copy in enumerate(copies):
+        copy.wait_send()
+        source = (me + count - 1 - n) % count
+        pltpu.make_async_remote_copy(
+            src_ref=own_ref, dst_ref=out_ref.at[source], send_sem=send_sem.at[n],
+            recv_sem=recv_sem.at[n], device_id={"slab": source}, device_id_type=MESH).wait_recv()
+    local.wait()
+
+
+def share(row, count):
+    return pl.pallas_call(
+        functools.partial(share_kernel, count),
+        out_shape=jax.ShapeDtypeStruct((count,) + row.shape, row.dtype),
+        in_specs=[pl.BlockSpec(memory_space=pltpu.VMEM)],
+        out_specs=pl.BlockSpec(memory_space=pltpu.VMEM),
+        scratch_shapes=[
+            pltpu.SemaphoreType.DMA,
+            pltpu.SemaphoreType.DMA((count - 1,)),
+            pltpu.SemaphoreType.DMA((count - 1,)),
+        ],
+        compiler_params=pltpu.CompilerParams(collective_id=2, has_side_effects=True),
+        name="share_scores",
+    )(row)
+
+
+GROUP = 8
+
+
+def score_kernel(pidx, ridx, half_ref, a_ref, b_ref, whi_ref, wlo_ref, cc_ref, pat_ref, out_ref):
+    step = pl.program_id(0)
+    lines = half_ref.shape[1]
+    f32, bf16 = jnp.float32, jnp.bfloat16
+    products = []
+    for e in range(GROUP):
+        spec = half_ref[pidx[step * GROUP + e]]
+        ref = ridx[step * GROUP + e]
+        products.append(a_ref[ref] * spec + b_ref[ref] * pltpu.roll(spec, 64, 1))
+    product = jnp.concatenate(products, axis=0)
+    hi = product.astype(bf16)
+    lo = (product - hi.astype(f32)).astype(bf16)
+    dot = lambda x, y: jnp.dot(x, y, preferred_element_type=f32)
+    turned = dot(hi, whi_ref[...]) + dot(lo, whi_ref[...]) + dot(hi, wlo_ref[...])
+    edge = jnp.concatenate([p[33:34] for p in products], axis=0).T
+    cosine, sine = pat_ref[0:1], pat_ref[1:2]
+    stacks = []
+    for e in range(GROUP):
+        rows = turned[e * lines:(e + 1) * lines]
+        er, ei = edge[0:lines, e:e + 1], edge[64:64 + lines, e:e + 1]
+        both = jnp.concatenate(
+            [rows[:, :128] + er * cosine - ei * sine, rows[:, 128:] + er * sine + ei * cosine], axis=0)
+        high = both.astype(bf16)
+        low = (both - high.astype(f32)).astype(bf16)
+        stacks.append(jnp.concatenate([high, low, high], axis=0))
+    peaks = []
+    for e in range(0, GROUP, 2):
+        shifts = jnp.abs(dot(cc_ref[...], jnp.concatenate(stacks[e:e + 2], axis=1)))
+        best = jnp.max(shifts, axis=0, keepdims=True)
+        peaks += [best[:, :128], best[:, 128:]]
+    peak = jnp.max(jnp.concatenate(peaks, axis=0), axis=1, keepdims=True)
+    out_ref[...] = jnp.broadcast_to(peak, (GROUP, 128))
+
+
+def score_tables(image_side, frequency_total, lines):
+    half = frequency_total // 2
+    x = np.arange(image_side)
+    freqs = np.arange(frequency_total) - half
+    ang = 2 * np.pi * ((freqs[:, None] * x[None, :]) % image_side) / image_side
+    cos, sin = np.cos(ang), np.sin(ang)
+    w = np.block([[cos, sin], [-sin, cos]]) / frequency_total
+    cr, sr = np.zeros((image_side, lines)), np.zeros((image_side, lines))
+    cr[:, : half + 1], sr[:, : half + 1] = cos[: half + 1].T, sin[: half + 1].T
+    c = np.concatenate([cr, -sr], axis=1)
+    def two(m):
+        high = m.astype(jnp.bfloat16)
+        return high, (m - high.astype(np.float64)).astype(jnp.bfloat16)
+    whi, wlo = two(w)
+    chi, clo = two(c)
+    pat = np.zeros((8, image_side), np.float32)
+    pat[0] = np.array([1, 0, -1, 0])[x % 4] / frequency_total
+    pat[1] = np.array([0, 1, 0, -1])[x % 4] / frequency_total
+    return whi, wlo, np.concatenate([chi, chi, clo], axis=1), pat
+
+
+def score_items(pidx, ridx, spectra, ref_a, ref_b, image_side, frequency_total):
+    slots = pidx.shape[0]
+    lines = spectra.shape[1]
+    whi, wlo, cc, pat = (jnp.asarray(t) for t in score_tables(image_side, frequency_total, lines))
+    full = lambda arr: pl.BlockSpec(arr.shape, lambda i, *_: (0,) * arr.ndim, pipeline_mode=pl.Buffered(1))
+    args = (spectra, ref_a, ref_b, whi, wlo, cc, pat)
+    return pl.pallas_call(
+        score_kernel,
+        out_shape=jax.ShapeDtypeStruct((slots, 128), jnp.float32),
+        grid_spec=pltpu.PrefetchScalarGridSpec(
+            num_scalar_prefetch=2, grid=(slots // GROUP,),
+            in_specs=[full(arr) for arr in args],
+            out_specs=pl.BlockSpec((GROUP, 128), lambda i, *_: (i, 0))),
+        compiler_params=pltpu.CompilerParams(vmem_limit_bytes=40 << 20),
+        name="score_items",
+    )(pidx, ridx, *args)
+
+
+def mirror_matrix(frequency_total):
+    turn = np.zeros((2 * frequency_total, 2 * frequency_total), np.float32)
+    for c in range(1, frequency_total):
+        turn[frequency_total - c, c] = 1.0
+        turn[2 * frequency_total - c, frequency_total + c] = -1.0
+    return turn
+
+
+def half_spectra(images, defocus, frequency_total, lines):
+    side = images.shape[-1]
+    half = frequency_total // 2
+    freqs = np.arange(frequency_total) - half
+    ang = 2 * np.pi * ((np.arange(side)[:, None] * freqs[None, :]) % side) / side
+    cos, sin = np.cos(ang).astype(np.float32), np.sin(ang).astype(np.float32)
+    first = jnp.einsum("pyx,xf->pyf", images, np.concatenate([cos, -sin], axis=1), precision=HALF_PRECISION)
+    both = jnp.concatenate(
+        [first, jnp.concatenate([first[..., frequency_total:], -first[..., :frequency_total]], axis=2)], axis=1)
+    rows = np.zeros((lines, 2 * side), np.float32)
+    rows[: half + 1] = np.concatenate([cos[:, : half + 1].T, sin[:, : half + 1].T], axis=1)
+    spectra = jnp.einsum("ry,pyg->prg", rows, both, precision=HALF_PRECISION)
+    edge_in = jnp.concatenate([first[:, :, 0], first[:, :, frequency_total]], axis=1)
+    back = np.zeros((side, frequency_total), np.float32), np.zeros((side, frequency_total), np.float32)
+    for r in range(1, half + 1):
+        back[0][:, r], back[1][:, r] = cos[:, frequency_total - r] if r < half else cos[:, half], (
+            sin[:, frequency_total - r] if r < half else sin[:, half])
+    edge = jnp.dot(edge_in, np.block([[back[0], back[1]], [back[1], -back[0]]]), precision=HALF_PRECISION)
+    f = freqs.astype(np.float32)
+    fr = np.zeros((lines,), np.float32)
+    fr[: half + 1] = f[: half + 1]
+    radius = (fr[:, None] ** 2 + f[None, :] ** 2) / float(half * half)
+    radius[half + 1] = radius[0]
+    radius[half + 1, 1:half + 1] = radius[0][(frequency_total - np.arange(1, half + 1)) % frequency_total]
+    phase = defocus[:, None, None] * radius[None]
+    factor = -(math.sqrt(1.0 - AMPLITUDE * AMPLITUDE) * jnp.sin(phase) + AMPLITUDE * jnp.cos(phase)) / side
+    value = spectra + edge[:, None, :] * (np.arange(lines) == half + 1).astype(np.float32)[None, :, None]
+    return value * jnp.concatenate([factor, factor], axis=2)
+
+
+def fold_references(references, lines):
+    frequency_total = references.shape[1]
+    half = frequency_total // 2
+    sign = np.concatenate([np.ones(frequency_total), -np.ones(frequency_total)]).astype(np.float32)
+    turned = jnp.einsum("rab,bc->rac", references[:, :half:-1], mirror_matrix(frequency_total) * sign[None, :],
+                        precision=HIGH_PRECISION)
+    folded = references[:, : half + 1] * sign
+    folded = folded + jnp.pad(turned, ((0, 0), (1, 1), (0, 0)))
+    edge = jnp.concatenate(
+        [jnp.pad(references[:, :half:-1, col], ((0, 0), (1, frequency_total - half)))
+         for col in (0, frequency_total)], axis=1)
+    folded = jnp.concatenate(
+        [folded, edge[:, None, :], jnp.zeros((references.shape[0], lines - half - 2, 2 * frequency_total))], axis=1)
+    re, im = folded[..., :frequency_total], folded[..., frequency_total:]
+    return jnp.concatenate([re, re], axis=2), jnp.concatenate([-im, im], axis=2)
+
+
+def gather_device(images, defocus, references, orient_owner, orient_local, block_owner, block_cell):
+    count = lax.axis_size("slab")
+    me = lax.axis_index("slab")
+    side = images.shape[-1]
+    frequency_total = references.shape[1]
+    half = frequency_total // 2
+    parts, picks = orient_owner.shape
+    refs, bands = block_cell.shape
+    items = parts * picks
+    cells = ZDEV * (VY // (frequency_total // bands)) * (VX // frequency_total)
+    band_rows = frequency_total // bands
+    cap = max(2, 2 * items // count)
+    lines = 40
+    meta_row = half + 2
+    own = half_spectra(images, defocus, frequency_total, lines)
+    ids = (orient_owner * refs + orient_local).astype(jnp.float32)
+    codes = (block_owner[..., 0] * cells + block_cell).astype(jnp.float32).reshape(parts, -1)
+    meta = jnp.concatenate([ids, codes], axis=1)
+    meta = jnp.pad(meta, ((0, 0), (0, 2 * frequency_total - meta.shape[1])))
+    own = jnp.where((jnp.arange(lines) == meta_row)[None, :, None], meta[:, None, :], own)
+    ref_a, ref_b = fold_references(references, lines)
+    gathered = ring_gather(own, count)
+    flat = gathered.reshape(count * parts, lines, 2 * frequency_total)
+    meta = flat[:, meta_row]
+    ids = meta[:, :picks].astype(jnp.int32)
+    codes = meta[:, picks:picks + refs * bands // parts].astype(jnp.int32).reshape(count * refs, bands)
+    by_source = ids.reshape(count, items)
+    owner = by_source // refs
+    same = owner[:, :, None] == owner[:, None, :]
+    before = np.tril(np.ones((items, items), bool), -1)
+    rank = jnp.sum(jnp.where(same & before[None], 1, 0), axis=2)
+    mine = (owner == me)[:, :, None] & (rank[:, :, None] == jnp.arange(cap)[None, None, :])
+    particle = (jnp.arange(count)[:, None] * parts + jnp.arange(items)[None, :] // picks)
+    pick = lambda value: jnp.sum(jnp.where(mine, value[:, :, None], 0), axis=1).reshape(-1)
+    pidx, ridx = pick(particle), pick(by_source % refs)
+    peaks = score_items(pidx, ridx, flat, ref_a, ref_b, side, frequency_total)[:, 0]
+    slot_scores = peaks * peaks + EPSILON
+    everyone = share(jnp.broadcast_to(slot_scores[None], (8, count * cap)), count)[:, 0]
+    table = everyone.reshape(count, count, cap).transpose(1, 0, 2).reshape(count, count * cap)
+    where = owner * cap + rank
+    scores = jnp.sum(
+        jnp.where(where[:, :, None] == jnp.arange(count * cap)[None, None, :], table[:, None, :], 0.0), axis=2)
+    scores = scores.reshape(count * parts, picks)
+    posterior = scores / jnp.sum(scores, axis=1, keepdims=True)
+    weight = jnp.zeros((count * refs, count * parts), jnp.float32)
+    for k in range(picks):
+        weight = weight + jnp.where(
+            jnp.arange(count * refs)[:, None] == ids[None, :, k], posterior[None, :, k], 0.0)
+    place = (codes.T[:, None, :] == (me * cells + jnp.arange(cells))[None, :, None]).astype(jnp.bfloat16)
+    w_hi = lax.reduce_precision(weight, 8, 7)
+    w_low = lax.reduce_precision(weight - w_hi, 8, 7)
+    mix = jnp.einsum("jcr,rp->jcp", place, jnp.concatenate([w_hi, w_low], axis=1).astype(jnp.bfloat16),
+                     preferred_element_type=jnp.float32)
+    n = count * parts
+    mix = mix[..., :n] + mix[..., n:]
+    halves = bands // 2
+    direct = jnp.einsum("jcp,pjil->cil", mix[:halves],
+                        flat[:, :half].reshape(n, halves, band_rows, 2 * frequency_total), precision=HALF_PRECISION)
+    mixed = mix[halves:][::-1]
+    back = jnp.einsum("jcp,pjil->cil", mixed,
+                      flat[:, 1:half + 1].reshape(n, halves, band_rows, 2 * frequency_total), precision=HALF_PRECISION)
+    edge = flat[:, half + 1].reshape(n, 2, frequency_total)[:, :, 1:half + 1].reshape(n, 2, halves, band_rows)
+    edge = jnp.einsum("jcp,ptji->cit", mixed, edge, precision=HALF_PRECISION)
+    back = jnp.einsum("cil,lm->cim", back, mirror_matrix(frequency_total), precision=HIGH_PRECISION)
+    lane = np.arange(2 * frequency_total)
+    back = back + jnp.where(lane == 0, edge[..., 0:1], 0.0) - jnp.where(lane == frequency_total, edge[..., 1:2], 0.0)
+    total = direct + back[:, ::-1]
+    row_blocks, col_blocks = VY // band_rows, VX // frequency_total
+    span = row_blocks // 2
+    total = total.reshape(ZDEV, 2, span, col_blocks, band_rows, 2 * frequency_total)
+    axis = lax.axis_index("dp")
+    mine_half = lax.dynamic_index_in_dim(total, axis, 1, keepdims=False)
+    peer_half = lax.dynamic_index_in_dim(total, 1 - axis, 1, keepdims=False)
+    summed = mine_half + lax.ppermute(peer_half, "dp", [(0, 1), (1, 0)])
+    summed = summed.reshape(ZDEV, span, col_blocks, band_rows, 2, frequency_total)
+    volume = summed.transpose(0, 1, 3, 4, 2, 5).reshape(ZDEV, span * band_rows, 2, col_blocks * frequency_total)
+    own_posterior = lax.dynamic_slice_in_dim(posterior, me * parts, parts, axis=0)
+    return (own_posterior, volume)
+
+
 def solution(mesh):
     in_specs = (
         P(("dp", "slab"), None, None),
@@ -223,6 +579,7 @@
         P("slab", None),
     )
     out_specs = (P(("dp", "slab"), None), P("slab", "dp", None, None))
+    small = mesh.shape["dp"] == 2 and mesh.shape["slab"] == 16
     return jax.shard_map(
-        per_device, mesh=mesh, in_specs=in_specs, out_specs=out_specs, check_vma=False
-    )
+        gather_device if small else per_device, mesh=mesh, in_specs=in_specs, out_specs=out_specs, check_vma=False
+    )

time: 352 us -> 159 us (0.45)
  waiting for transfers between devices: 161 us -> 23.2 us
  Pallas kernels: 0 us -> 54.6 us
  starting transfers between devices: 46.1 us -> 1.5 us
  local copies, waits for them, and re-layouts: 79.6 us -> 39.1 us
  between operations: 14.4 us -> 1.13 us
  matrix products: 39.3 us -> 29.4 us
    all_to_all x6 -> x0, waiting for transfers between devices: 123 us -> none  [the longest x1 73.1 us: per_device(): lax.all_to_all(send_spectra.reshape(owner_count, slot_cap, frequency_tota...]
    pallas_call x0 -> x3, Pallas kernels: none -> 54.6 us  [the longest x1 33.6 us: ring_gather(): pl.pallas_call(functools.partial(gather_kernel, chips), out_shape=jax.Sha...]
    all_to_all x6 -> x0, starting transfers between devices: 46.1 us -> none  [the longest x1 19.6 us: per_device(): lax.all_to_all(slot_scores, 'slab', split_axis=0, concat_axis=0, tiled=True)]
    reduce_scatter x1 -> x0, waiting for transfers between devices: 37.8 us -> none  [per_device(): lax.psum_scatter(partial_value, 'dp', scatter_dimension=1, tiled=True)]
    scatter x5 -> x0, local copies, waits for them, and re-layouts: 35.5 us -> none  [the longest x1 23.9 us: per_device(): block_send = jnp.zeros((owner_count * block_cap, band_rows, 2 * frequency...]
    ppermute x0 -> x1, waiting for transfers between devices: none -> 23.2 us  [gather_device(): summed = mine_half + lax.ppermute(peer_half, 'dp', [(0, 1), (1, 0)])]
    squeeze x8 -> x0, local copies, waits for them, and re-layouts: 10.2 us -> none  [score_slots(): return lax.map(one_group, grouped).reshape(-1)]
    dot_general x21 -> x10, matrix products: 39.3 us -> 29.4 us  [the longest x1 8.96 us: gather_device(): jnp.einsum('jcp,pjil->cil', mixed, flat[:, 1:half + 1].reshape(n, halves,...]
  transfers between devices with their start and end apart: 7 -> 1, of which waited for: 5 -> 1; matrix products, arithmetic and copies ran while one was open for 17% -> 0% of each run, Pallas kernels for 0% -> 0%
where the time goes in v1:
time: 159 us
  Pallas kernels  54.6 us (34%)
  local copies, waits for them, and re-layouts  39.1 us (25%)
  matrix products  29.4 us (18%)
  waiting for transfers between devices  23.2 us (15%)
  other arithmetic  9.64 us (6%)
    pallas_call x1, Pallas kernels, ring_gather(): pl.pallas_call(functools.partial(gather_kernel, chips), out_shape=jax.Sha...  33.6 us
    ppermute x1, waiting for transfers between devices, gather_device(): summed = mine_half + lax.ppermute(peer_half, 'dp', [(0, 1), (1, 0)])  23.2 us
    unnamed x63, local copies, waits for them, and re-layouts  14.5 us
    pallas_call x1, Pallas kernels, score_items(): pl.pallas_call(score_kernel, out_shape=jax.ShapeDtypeStruct((slots, 128),...  12.4 us
    dot_general x1, matrix products, gather_device(): jnp.einsum('jcp,pjil->cil', mixed, flat[:, 1:half + 1].reshape(n, halves,...  8.96 us
    pallas_call x1, Pallas kernels, share(): pl.pallas_call(functools.partial(share_kernel, count), out_shape=jax.Shap...  8.58 us
    reshape x1, local copies, waits for them, and re-layouts, gather_device(): flat[:, :half].reshape(n, halves, band_rows, 2 * frequency_total)  8.44 us
    dot_general x1, matrix products, gather_device(): jnp.einsum('jcp,pjil->cil', mix[:halves], flat[:, :half].reshape(n, halve...  7.61 us
  transfers between devices with their start and end apart: 1, of which 1 were waited for; matrix products, arithmetic and copies ran while one was open for 0% of the time, Pallas kernels for 0%

profile of v1, /device:TPU:0, one launch (start us, length us, event | category | flops | bytes accessed | tf_op | source)
XLA Modules:
  0.0 158.6 jit_solution(10650819431714523337)
XLA Ops:
  0.7 1.2 copy-done
  1.9 1.4 convolution_bitcast_fusion
  3.3 1.0 fusion.58
  5.5 1.3 fusion.56
  6.8 0.8 slice.106
  8.0 1.3 fusion.45
  9.6 3.0 %fusion.32.own_ref = f32[16,40,128]{2,1,0:T(8,128)} fusion(f32[40,256,1]{1,0,2:T(8,128)S(1)} %copy-done.27, f32[16,128,64]{1,2,0:T(8,128)} %get-tuple-element.33, f32[16,128,64]{1,2,0:T(8,128)} %get-tuple-element.32, f32[16,128,128]{1,2,0:T(8,128)S(1)} %convolution_bitcast_fusion, f32[16,40,64]{2,1,0:T(8,128)S(1)} %fusion.45, f32[40]{0:T(128)S(1)} %copy-done.28, ...), kind=kOutput, calls=%fused_computation.30 | convolution fusion | flops 127287296 | bytes 2646216 | tf_op jit(solution)/shard_map/ry,pyg->prg/dot_general | solution.py:455
  12.6 33.6 %ring_gather.1 = f32[16,16,40,128]{3,2,1,0:T(8,128)} custom-call(f32[16,40,128]{2,1,0:T(8,128)} %fusion.32.own_ref), custom_call_target="tpu_custom_call" | custom-call | tf_op jit(solution)/shard_map/ring_gather/pallas_call | solution.py:302
  46.2 1.9 %fusion.55 = (f32[256,1,128]{2,1,0:T(1,128)S(1)}, f32[256,1,128]{2,1,0:T(1,128)S(1)}) fusion(f32[256,40,128]{2,1,0:T(8,128)} %bitcast.94), kind=kLoop, calls=%fused_computation.115 | loop fusion | bytes 524288 | tf_op jit(solution)/shard_map/slice | solution.py:552
  48.7 8.4 %slice_bitcast_fusion.1 = (f32[256,4,8,128]{3,2,1,0:T(8,128)}, f32[256,4,8,128]{3,2,1,0:T(8,128)}) fusion(f32[256,40,128]{2,1,0:T(8,128)} %bitcast.95), kind=kLoop, calls=%fused_computation.3 | loop fusion | bytes 16777216 | tf_op jit(solution)/shard_map/reshape | solution.py:548
  58.6 1.3 copy.114
  61.2 0.8 pad_add_fusion
  63.4 2.5 %copy-done.1 = f32[16,16,40,128]{3,2,1,0:T(8,128)S(1)} copy-done((f32[16,16,40,128]{3,2,1,0:T(8,128)S(1)}, f32[16,16,40,128]{3,2,1,0:T(8,128)}, u32[]{:S(2)}) %copy-start.1) | copy-done | bytes 5242904
  65.9 12.4 %score_items.1 = f32[128,128]{1,0:T(8,128)S(1)} custom-call(s32[128]{0:T(128)S(1)} %reshape.250.pidx, s32[128]{0:T(128)S(1)} %reshape.251.ridx, f32[256,40,128]{2,1,0:T(8,128)S(1)} %bitcast.96, f32[32,40,128]{2,1,0:T(8,128)S(1)} %get-tuple-element.43.a_ref, f32[32,40,128]{2,1,0:T(8,128)S(1)} %get-tuple-element.44.b_ref, bf16[128,256]{1,0:T(8,128)(2,1)S(1)} %copy-done.2, ...), custom_call_target="tpu_custom_call" | custom-call | tf_op jit(solution)/shard_map/score_items/pallas_call | solution.py:424
  79.0 8.6 %share_scores.1 = f32[16,8,128]{2,1,0:T(8,128)} custom-call(f32[8,128]{1,0:T(8,128)} %broadcast_in_dim.167.own_ref), custom_call_target="tpu_custom_call" | custom-call | tf_op jit(solution)/shard_map/share_scores/pallas_call | solution.py:345
  87.6 0.8 slice.112
  90.3 2.4 %fusion = f32[8,512,512]{2,1,0:T(8,128)S(1)} fusion(s32[8,512]{1,0:T(8,128)S(1)} %copy.99, s32[512]{0:T(512)S(1)} %iota_add_fusion, bf16[512,256]{1,0:T(8,128)(2,1)S(1)} %get-tuple-element.40, bf16[512,256]{1,0:T(8,128)(2,1)S(1)} %get-tuple-element.39), kind=kOutput, calls=%fused_computation | convolution fusion | flops 2150629376 | bytes 8931328 | tf_op jit(solution)/shard_map/jcr,rp->jcp/dot_general | solution.py:542
  93.3 1.9 %copy-done.6 = f32[8,512,256]{2,1,0:T(8,128)} copy-done((f32[8,512,256]{2,1,0:T(8,128)}, f32[8,512,256]{2,1,0:T(8,128)S(1)}, u32[]{:S(2)}) %copy-start.6) | copy-done | bytes 4194328
  95.2 1.5 slice.156
  96.7 1.7 %rev.18 = f32[4,512,256]{2,1,0:T(8,128)S(1)} reverse(f32[4,512,256]{2,1,0:T(8,128)} %slice.156), dimensions={0} | reverse | bytes 4194304 | tf_op jit(solution)/shard_map/rev | solution.py:549
  98.5 0.9 fusion.35
  99.5 9.0 %fusion.2 = f32[512,8,128,1]{2,0,3,1:T(8,128)} fusion(f32[256,4,8,128]{3,2,1,0:T(8,128)} %get-tuple-element.23, f32[4,512,256]{2,1,0:T(8,128)S(1)} %rev.18), kind=kOutput, calls=%fused_computation.5 | convolution fusion | flops 3221225472 | bytes 8388608 | tf_op jit(solution)/shard_map/jcp,pjil->cil/dot_general | solution.py:550
  108.5 4.3 %select_subtract_fusion = f32[512,8,128]{2,0,1:T(8,128)S(1)} fusion(f32[128,128,1]{1,0,2:T(8,128)S(1)} %copy-done.12, f32[512,8,128,1]{2,0,3,1:T(8,128)} %fusion.2, f32[512,8]{0,1:T(8,128)S(1)} %get-tuple-element.38, f32[512,8]{0,1:T(8,128)S(1)} %get-tuple-element.37, pred[128]{0:T(512)(128)(4,1)S(1)} %copy-done.24, pred[128]{0:T(512)(128)(4,1)S(1)} %copy-done.23), kind=kOutput, calls=%fused_computation.24 | convolution fusion | flops 807403520 | bytes 4292864 | tf_op jit(solution)/shard_map/cil,lm->cim/dot_general | solution.py:554
  112.8 7.6 %bitcast_add_fusion = f32[512,8,128]{2,0,1:T(8,128)S(1)} fusion(f32[512,8,128]{2,0,1:T(8,128)S(1)} %select_subtract_fusion, f32[256,4,8,128]{3,2,1,0:T(8,128)} %get-tuple-element.22, f32[8,512,256]{2,1,0:T(8,128)S(1)} %copy-done.7), kind=kOutput, calls=%fused_computation.23 | convolution fusion | flops 3221749760 | bytes 10485760 | tf_op jit(solution)/shard_map/jcp,pjil->cil/dot_general | solution.py:547
  120.4 1.1 constant_dynamic-slice_fusion.1
  121.5 1.6 copy.124
  123.1 1.5 collective-permute-start
  125.3 23.2 %collective-permute-done = f32[4,16,4,8,128]{4,3,2,1,0:T(8,128)S(1)} collective-permute-done((f32[4,16,4,8,128]{4,3,2,1,0:T(8,128)}, f32[4,16,4,8,128]{4,3,2,1,0:T(8,128)S(1)}, u32[]{:S(2)}, u32[]{:S(2)}) %collective-permute-start) | collective-permute-done | bytes 1048608 | tf_op jit(solution)/shard_map/ppermute | solution.py:564
  148.5 1.6 %bitcast_add_fusion.1 = f32[4,16,4,8,128]{4,3,2,1,0:T(8,128)} fusion(f32[4,16,4,8,128]{4,3,2,1,0:T(8,128)S(1)} %collective-permute-done, f32[4,1,16,4,8,128]{5,3,2,1,0,4:T(4,128)S(1)} %copy-done.9), kind=kLoop, calls=%fused_computation.33 | loop fusion | flops 262144 | bytes 3145728 | tf_op jit(solution)/shard_map/add | solution.py:564
  150.1 2.5 %reshape.258 = f32[4,16,4,8,2,64]{5,4,3,2,1,0:T(2,128)S(1)} reshape(f32[4,16,4,8,128]{4,3,2,1,0:T(8,128)} %bitcast_add_fusion.1) | data formatting | bytes 2097152 | tf_op jit(solution)/shard_map/reshape | solution.py:565
  152.6 2.3 %copy.112 = f32[4,16,8,2,4,64]{5,4,3,2,1,0:T(4,128)} copy(f32[4,16,8,2,4,64]{5,3,2,4,1,0:T(2,128)S(1)} %bitcast.98) | data formatting | bytes 2097152
  154.9 3.7 %reshape.270 = f32[4,128,2,256]{3,2,1,0:T(2,128)} reshape(f32[4,16,8,2,4,64]{5,4,3,2,1,0:T(4,128)} %copy.112) | data formatting | bytes 2097152
  (108 shorter events, 10.2 us)
Async XLA Ops:
  0.6 1.2 copy-start
  0.6 4.9 %copy-start.8 = (f32[32,64,128]{2,1,0:T(8,128)S(1)}, f32[32,64,128]{2,1,0:T(8,128)}, u32[]{:S(2)}) copy-start(f32[32,64,128]{2,1,0:T(8,128)} %param.24) | copy-start | bytes 3145732
  4.3 3.3 %copy-start.18 = (s32[32,8]{0,1:T(8,128)S(1)}, s32[32,8]{0,1:T(8,128)}, u32[]{:S(2)}) copy-start(s32[32,8]{0,1:T(8,128)} %param.28) | copy-start | bytes 3076
  4.4 3.3 %copy-start.19 = (s32[32,8,1]{0,2,1:T(1,128)S(1)}, s32[32,8,1]{0,2,1:T(1,128)}, u32[]{:S(2)}) copy-start(s32[32,8,1]{0,2,1:T(1,128)} %param.27) | copy-start | bytes 3076
  4.4 3.4 %copy-start.20 = (s32[16,4]{0,1:T(4,128)S(1)}, s32[16,4]{0,1:T(4,128)}, u32[]{:S(2)}) copy-start(s32[16,4]{0,1:T(4,128)} %param.26) | copy-start | bytes 772
  4.4 3.4 %copy-start.21 = (s32[16,4]{0,1:T(4,128)S(1)}, s32[16,4]{0,1:T(4,128)}, u32[]{:S(2)}) copy-start(s32[16,4]{0,1:T(4,128)} %param.25) | copy-start | bytes 772
  4.4 3.5 %copy-start.14 = (f32[128,128]{1,0:T(8,128)S(1)}, f32[128,128]{1,0:T(8,128)}, u32[]{:S(2)}) copy-start(f32[128,128]{1,0:T(8,128)} %constant.144) | copy-start | bytes 196612
  4.4 3.7 %copy-start.16 = (f32[40,64]{1,0:T(8,128)S(1)}, f32[40,64]{1,0:T(8,128)}, u32[]{:S(2)}) copy-start(f32[40,64]{1,0:T(8,128)} %constant.147) | copy-start | bytes 30724
  4.4 3.7 %copy-start.22 = (f32[16]{0:T(128)S(1)}, f32[16]{0:T(128)}, u32[]{:S(2)}) copy-start(f32[16]{0:T(128)} %param.23) | copy-start | bytes 196
  4.4 5.0 %copy-start.15 = (f32[128,128]{1,0:T(8,128)S(1)}, f32[128,128]{1,0:T(8,128)}, u32[]{:S(2)}) copy-start(f32[128,128]{1,0:T(8,128)} %constant.145) | copy-start | bytes 196612
  4.4 5.1 %copy-start.27 = (f32[40,256,1]{1,0,2:T(8,128)S(1)}, f32[40,256,1]{1,0,2:T(8,128)}, u32[]{:S(2)}) copy-start(f32[40,256,1]{1,0,2:T(8,128)} %constant.150) | copy-start | bytes 122884
  4.4 5.1 %copy-start.28 = (f32[40]{0:T(128)S(1)}, f32[40]{0:T(128)}, u32[]{:S(2)}) copy-start(f32[40]{0:T(128)} %constant.146) | copy-start | bytes 484
  48.7 8.5 %copy-start.17 = (pred[64,64]{1,0:T(32,128)(4,1)S(1)}, pred[64,64]{1,0:T(32,128)(4,1)}, u32[]{:S(2)}) copy-start(pred[64,64]{1,0:T(32,128)(4,1)} %constant.148) | copy-start | bytes 12292
  48.7 9.0 %copy-start.25 = (s32[64]{0:T(128)S(1)}, s32[64]{0:T(128)}, u32[]{:S(2)}) copy-start(s32[64]{0:T(128)} %and_select_fusion) | copy-start | bytes 772
  48.7 9.0 %copy-start.26 = (s32[16]{0:T(128)S(1)}, s32[16]{0:T(128)}, u32[]{:S(2)}) copy-start(s32[16]{0:T(128)} %iota_multiply_fusion) | copy-start | bytes 196
  48.7 11.3 %copy-start.11 = (f32[32,31,1]{2,1,0:T(8,128)S(1)}, f32[32,31,1]{2,1,0:T(8,128)}, u32[]{:S(2)}) copy-start(f32[32,31,1]{2,1,0:T(8,128)} %get-tuple-element.29) | copy-start | bytes 11908
  48.7 11.7 %copy-start.10 = (f32[32,31,128]{2,1,0:T(8,128)S(1)}, f32[32,31,128]{2,1,0:T(8,128)}, u32[]{:S(2)}) copy-start(f32[32,31,128]{2,1,0:T(8,128)} %slice.106) | copy-start | bytes 1523716
  57.2 3.5 %copy-start.13 = (f32[128,128,1]{1,0,2:T(8,128)S(1)}, f32[128,128,1]{1,0,2:T(8,128)}, u32[]{:S(2)}) copy-start(f32[128,128,1]{1,0,2:T(8,128)} %constant.151) | copy-start | bytes 196612
  62.5 0.8 copy-start.2
  62.5 0.9 copy-start.3
  62.5 0.9 copy-start.4
  62.5 0.9 copy-start.5
  63.4 2.5 %copy-start.1 = (f32[16,16,40,128]{3,2,1,0:T(8,128)S(1)}, f32[16,16,40,128]{3,2,1,0:T(8,128)}, u32[]{:S(2)}) copy-start(f32[16,16,40,128]{3,2,1,0:T(8,128)} %ring_gather.1) | copy-start | bytes 15728644
  93.3 1.9 %copy-start.6 = (f32[8,512,256]{2,1,0:T(8,128)}, f32[8,512,256]{2,1,0:T(8,128)S(1)}, u32[]{:S(2)}) copy-start(f32[8,512,256]{2,1,0:T(8,128)S(1)} %slice_add_fusion) | copy-start | bytes 12582916
  99.5 9.0 %copy-start.12 = (f32[128,128,1]{1,0,2:T(8,128)S(1)}, f32[128,128,1]{1,0,2:T(8,128)}, u32[]{:S(2)}) copy-start(f32[128,128,1]{1,0,2:T(8,128)} %constant.152) | copy-start | bytes 196612
  99.5 9.0 %copy-start.23 = (pred[128]{0:T(512)(128)(4,1)S(1)}, pred[128]{0:T(512)(128)(4,1)}, u32[]{:S(2)}) copy-start(pred[128]{0:T(512)(128)(4,1)} %constant.130.clone) | copy-start | bytes 388
  99.5 9.0 %copy-start.24 = (pred[128]{0:T(512)(128)(4,1)S(1)}, pred[128]{0:T(512)(128)(4,1)}, u32[]{:S(2)}) copy-start(pred[128]{0:T(512)(128)(4,1)} %constant.131.clone) | copy-start | bytes 388
  108.5 4.3 %copy-start.7 = (f32[8,512,256]{2,1,0:T(8,128)S(1)}, f32[8,512,256]{2,1,0:T(8,128)}, u32[]{:S(2)}) copy-start(f32[8,512,256]{2,1,0:T(8,128)} %copy-done.6) | copy-start | bytes 12582916
  121.5 27.0 %copy-start.9 = (f32[4,1,16,4,8,128]{5,3,2,1,0,4:T(4,128)S(1)}, f32[4,1,16,4,8,128]{5,3,2,1,0,4:T(4,128)}, u32[]{:S(2)}) copy-start(f32[4,1,16,4,8,128]{5,3,2,1,0,4:T(4,128)} %get-tuple-element.26) | copy-start | bytes 3145732
  123.1 25.4 %collective-permute-start = (f32[4,16,4,8,128]{4,3,2,1,0:T(8,128)}, f32[4,16,4,8,128]{4,3,2,1,0:T(8,128)S(1)}, u32[]{:S(2)}, u32[]{:S(2)}) collective-permute-start(f32[4,16,4,8,128]{4,3,2,1,0:T(8,128)} %bitcast.92), channel_id=1, source_target_pairs={{0,16},{16,0},{1,17},{17,1},{2,18},{18,2},{3,19},{19,3},{4,20},{20... | collective-permute-start | bytes 3145736 | tf_op jit(solution)/shard_map/ppermute | solution.py:564

commit v2 on v1

--- a/solution.py
+++ b/solution.py
@@ -486,6 +486,130 @@
         [folded, edge[:, None, :], jnp.zeros((references.shape[0], lines - half - 2, 2 * frequency_total))], axis=1)
     re, im = folded[..., :frequency_total], folded[..., frequency_total:]
     return jnp.concatenate([re, re], axis=2), jnp.concatenate([-im, im], axis=2)
+
+
+def volume_kernel(cidx_ref, post_ref, flat_ref, turn_ref, out_ref,
+                  s_hi, s_lo, m_hi, m_lo, edge, away, inbox, send_sem, recv_sem):
+    f32, bf16 = jnp.float32, jnp.bfloat16
+    picks, n = post_ref.shape
+    lines = flat_ref.shape[0] // n
+    bands, halves = m_hi.shape[1], m_hi.shape[1] // 2
+    peer = 1 - lax.axis_index("dp")
+    barrier = pltpu.get_barrier_semaphore()
+    pl.semaphore_signal(barrier, inc=1, device_id={"dp": peer}, device_id_type=MESH)
+
+    def split(value):
+        high = value.astype(bf16)
+        return high, (value - high.astype(f32)).astype(bf16)
+
+    for row in range(s_hi.shape[0]):
+        s_hi[row], s_lo[row] = split(flat_ref[pl.ds(row, n, stride=lines), :])
+
+    def build(j, carry):
+        where = cidx_ref[pl.ds(j, 1), :]
+        for part in range(2):
+            cell = lax.broadcasted_iota(jnp.int32, (n, n), 0) + part * n
+            total = jnp.zeros((n, n), f32)
+            for k in range(picks):
+                total = total + jnp.where(where[:, k * n:(k + 1) * n] == cell, post_ref[k:k + 1, :], 0.0)
+            m_hi[part, j], m_lo[part, j] = split(total)
+        return carry
+
+    lax.fori_loop(0, bands, build, 0)
+    pl.semaphore_wait(barrier, 1)
+
+    def dot(x, y):
+        return jnp.dot(x, y, preferred_element_type=f32)
+
+    def product(part, j, hi, lo):
+        return dot(m_hi[part, j], hi) + dot(m_lo[part, j], hi) + dot(m_hi[part, j], lo)
+
+    last = s_hi.shape[0] - 1
+    lane = lax.broadcasted_iota(jnp.int32, (n, 128), 1)
+
+    def edges(part):
+        total = jnp.zeros((n, 128), f32)
+        ext = flat_ref[pl.ds(last, n, stride=lines), :]
+        for jj in range(halves):
+            hi, lo = split(pltpu.roll(ext, 128 - (1 + 8 * jj), 1))
+            total = total + product(part, bands - 1 - jj, hi, lo)
+        edge[...] = total
+
+    def pair(ref, first, second):
+        return jnp.concatenate([ref[first], ref[second]], axis=1)
+
+    def chunk(part, ip):
+        i = 2 * ip
+        front, back = jnp.zeros((n, 256), f32), jnp.zeros((n, 256), f32)
+        for jj in range(halves):
+            a, b = 8 * jj + i, 8 * jj + i + 1
+            front = front + product(part, jj, pair(s_hi, a, b), pair(s_lo, a, b))
+            a, b = 8 * jj + 8 - i, 8 * jj + 7 - i
+            back = back + product(part, bands - 1 - jj, pair(s_hi, a, b), pair(s_lo, a, b))
+        result = []
+        for u in range(2):
+            hi, lo = split(back[:, u * 128:(u + 1) * 128])
+            flipped = dot(hi, turn_ref[...]) + dot(lo, turn_ref[...])
+            at = pltpu.roll(edge[...], (128 - (7 - i - u)) % 128, 1)
+            flipped = flipped + jnp.where(lane == 0, at, jnp.where(lane == 64, -at, 0.0))
+            full = front[:, u * 128:(u + 1) * 128] + flipped
+            rolled = pltpu.roll(full, 64, 1)
+            q = n // 4
+            low = lane[:q] < 64
+            for p in range(2):
+                x, y = slice(2 * p * q, (2 * p + 1) * q), slice((2 * p + 1) * q, (2 * p + 2) * q)
+                result.append((u, p, jnp.where(low, full[x], rolled[y])))
+                result.append((u, 2 + p, jnp.where(low, rolled[x], full[y])))
+        return result
+
+    def copy_of(ip):
+        return pltpu.make_async_remote_copy(
+            src_ref=away.at[ip], dst_ref=inbox.at[ip], send_sem=send_sem.at[ip], recv_sem=recv_sem.at[ip],
+            device_id={"dp": peer}, device_id_type=MESH)
+
+    pieces = away.shape[0]
+    edges(0)
+    for ip in range(pieces):
+        for u, p, value in chunk(0, ip):
+            away[ip, u, p] = value
+        copy_of(ip).start()
+    edges(1)
+    for ip in range(pieces):
+        for u, p, value in chunk(1, ip):
+            out_ref[ip, u, p] = value
+    for ip in range(pieces):
+        copy_of(ip).wait_recv()
+        out_ref[ip] = out_ref[ip] + inbox[ip]
+    for ip in range(pieces):
+        copy_of(ip).wait_send()
+
+
+def build_volume(cidx, post, flat, half):
+    bands, n = cidx.shape[0], post.shape[1]
+    lanes = flat.shape[1]
+    turn = jnp.asarray(mirror_matrix(lanes // 2), jnp.bfloat16)
+    piece = (4, 2, 4, n // 4, lanes)
+    vmem = pl.BlockSpec(memory_space=pltpu.VMEM)
+    return pl.pallas_call(
+        volume_kernel,
+        out_shape=jax.ShapeDtypeStruct(piece, jnp.float32),
+        in_specs=[vmem] * 4,
+        out_specs=vmem,
+        scratch_shapes=[
+            pltpu.VMEM((half + 2, n, lanes), jnp.bfloat16),
+            pltpu.VMEM((half + 2, n, lanes), jnp.bfloat16),
+            pltpu.VMEM((2, bands, n, n), jnp.bfloat16),
+            pltpu.VMEM((2, bands, n, n), jnp.bfloat16),
+            pltpu.VMEM((n, lanes), jnp.float32),
+            pltpu.VMEM(piece, jnp.float32),
+            pltpu.VMEM(piece, jnp.float32),
+            pltpu.SemaphoreType.DMA((4,)),
+            pltpu.SemaphoreType.DMA((4,)),
+        ],
+        compiler_params=pltpu.CompilerParams(
+            collective_id=3, has_side_effects=True, vmem_limit_bytes=48 << 20),
+        name="build_volume",
+    )(cidx, post, flat, turn)
 
 
 def gather_device(images, defocus, references, orient_owner, orient_local, block_owner, block_cell):
@@ -532,38 +656,21 @@
         jnp.where(where[:, :, None] == jnp.arange(count * cap)[None, None, :], table[:, None, :], 0.0), axis=2)
     scores = scores.reshape(count * parts, picks)
     posterior = scores / jnp.sum(scores, axis=1, keepdims=True)
-    weight = jnp.zeros((count * refs, count * parts), jnp.float32)
-    for k in range(picks):
-        weight = weight + jnp.where(
-            jnp.arange(count * refs)[:, None] == ids[None, :, k], posterior[None, :, k], 0.0)
-    place = (codes.T[:, None, :] == (me * cells + jnp.arange(cells))[None, :, None]).astype(jnp.bfloat16)
-    w_hi = lax.reduce_precision(weight, 8, 7)
-    w_low = lax.reduce_precision(weight - w_hi, 8, 7)
-    mix = jnp.einsum("jcr,rp->jcp", place, jnp.concatenate([w_hi, w_low], axis=1).astype(jnp.bfloat16),
-                     preferred_element_type=jnp.float32)
     n = count * parts
-    mix = mix[..., :n] + mix[..., n:]
-    halves = bands // 2
-    direct = jnp.einsum("jcp,pjil->cil", mix[:halves],
-                        flat[:, :half].reshape(n, halves, band_rows, 2 * frequency_total), precision=HALF_PRECISION)
-    mixed = mix[halves:][::-1]
-    back = jnp.einsum("jcp,pjil->cil", mixed,
-                      flat[:, 1:half + 1].reshape(n, halves, band_rows, 2 * frequency_total), precision=HALF_PRECISION)
-    edge = flat[:, half + 1].reshape(n, 2, frequency_total)[:, :, 1:half + 1].reshape(n, 2, halves, band_rows)
-    edge = jnp.einsum("jcp,ptji->cit", mixed, edge, precision=HALF_PRECISION)
-    back = jnp.einsum("cil,lm->cim", back, mirror_matrix(frequency_total), precision=HIGH_PRECISION)
-    lane = np.arange(2 * frequency_total)
-    back = back + jnp.where(lane == 0, edge[..., 0:1], 0.0) - jnp.where(lane == frequency_total, edge[..., 1:2], 0.0)
-    total = direct + back[:, ::-1]
     row_blocks, col_blocks = VY // band_rows, VX // frequency_total
     span = row_blocks // 2
-    total = total.reshape(ZDEV, 2, span, col_blocks, band_rows, 2 * frequency_total)
-    axis = lax.axis_index("dp")
-    mine_half = lax.dynamic_index_in_dim(total, axis, 1, keepdims=False)
-    peer_half = lax.dynamic_index_in_dim(total, 1 - axis, 1, keepdims=False)
-    summed = mine_half + lax.ppermute(peer_half, "dp", [(0, 1), (1, 0)])
-    summed = summed.reshape(ZDEV, span, col_blocks, band_rows, 2, frequency_total)
-    volume = summed.transpose(0, 1, 3, 4, 2, 5).reshape(ZDEV, span * band_rows, 2, col_blocks * frequency_total)
+    cell = codes - me * cells
+    z, rb, cb = cell // (row_blocks * col_blocks), cell // col_blocks % row_blocks, cell % col_blocks
+    order = (jnp.where(rb // span == lax.axis_index("dp"), 1, 0) * (cells // 2)
+             + cb * (ZDEV * span) + z * span + rb % span + 1)
+    order = jnp.where((cell >= 0) & (cell < cells), order, 0).T
+    named = (jnp.arange(count * refs)[:, None] == ids.T.reshape(-1)[None, :]).astype(jnp.bfloat16)
+    digits = jnp.concatenate([order // 32, order % 32], axis=0).astype(jnp.bfloat16)
+    digits = jnp.dot(digits, named, preferred_element_type=jnp.float32).astype(jnp.int32)
+    cidx = digits[:bands] * 32 + digits[bands:] - 1
+    built = build_volume(cidx, posterior.T, flat.reshape(n * lines, 2 * frequency_total), half)
+    built = built.reshape(band_rows, 2, 2, ZDEV, span, 2 * frequency_total)
+    volume = built.transpose(3, 4, 0, 1, 2, 5).reshape(ZDEV, span * band_rows, 2, col_blocks * frequency_total)
     own_posterior = lax.dynamic_slice_in_dim(posterior, me * parts, parts, axis=0)
     return (own_posterior, volume)
 

time: 159 us -> 117 us (0.74)
  Pallas kernels: 54.6 us -> 87 us
  matrix products: 29.4 us -> 4.5 us
  local copies, waits for them, and re-layouts: 39.1 us -> 14.4 us
  waiting for transfers between devices: 23.2 us -> 0 us
    pallas_call x0 -> x1, Pallas kernels: none -> 32.5 us  [build_volume(): pl.pallas_call(volume_kernel, out_shape=jax.ShapeDtypeStruct(piece, jnp.f...]
    dot_general x5 -> x1, matrix products: 24.1 us -> 0.46 us  [gather_device(): jnp.dot(digits, named, preferred_element_type=jnp.float32).astype(jnp.int32)]
    ppermute x1 -> x0, waiting for transfers between devices: 23.2 us -> none  [gather_device(): summed = mine_half + lax.ppermute(peer_half, 'dp', [(0, 1), (1, 0)])]
    unnamed x63 -> x35, local copies, waits for them, and re-layouts: 14.5 us -> 4.2 us
    reshape x3 -> x1, local copies, waits for them, and re-layouts: 11 us -> 2.17 us  [gather_device(): built.transpose(3, 4, 0, 1, 2, 5)]
    slice x5 -> x1, local copies, waits for them, and re-layouts: 4.18 us -> 1.34 us  [gather_device(): meta = flat[:, meta_row]]
    dynamic_slice x2 -> x0, local copies, waits for them, and re-layouts: 2.7 us -> none  [the longest x1 1.58 us: gather_device(): peer_half = lax.dynamic_index_in_dim(total, 1 - axis, 1, keepdims=False)]
    add x3 -> x0, other arithmetic: 2.15 us -> none  [the longest x1 1.6 us: gather_device(): summed = mine_half + lax.ppermute(peer_half, 'dp', [(0, 1), (1, 0)])]
  transfers between devices with their start and end apart: 1 -> 0, of which waited for: 1 -> 0; matrix products, arithmetic and copies ran while one was open for 0% -> 0% of each run, Pallas kernels for 0% -> 0%
where the time goes in v2:
time: 117 us; the launch traced here: 116 us
  Pallas kernels  87 us (74%)
  local copies, waits for them, and re-layouts  14.4 us (12%)
  other arithmetic  9.4 us (8%)
  matrix products  4.5 us (4%)
    pallas_call x1, Pallas kernels, ring_gather(): pl.pallas_call(functools.partial(gather_kernel, chips), out_shape=jax.Sha...  33.7 us
    pallas_call x1, Pallas kernels, build_volume(): pl.pallas_call(volume_kernel, out_shape=jax.ShapeDtypeStruct(piece, jnp.f...  32.5 us
    pallas_call x1, Pallas kernels, score_items(): pl.pallas_call(score_kernel, out_shape=jax.ShapeDtypeStruct((slots, 128),...  12.2 us
    pallas_call x1, Pallas kernels, share(): pl.pallas_call(functools.partial(share_kernel, count), out_shape=jax.Shap...  8.56 us
    unnamed x35, local copies, waits for them, and re-layouts  4.2 us

profile of v2, /device:TPU:0, one launch (start us, length us, event | category | flops | bytes accessed | tf_op | source)
XLA Modules:
  0.0 116.4 jit_solution(1302618834120927790)
XLA Ops:
  0.7 0.5 iota_compare_fusion.9
  1.3 0.6 and_select_fusion
  1.9 0.7 add_convert_fusion
  2.6 0.7 fusion.55
  3.6 2.0 %fusion.24 = f32[16,40,64]{2,1,0:T(8,128)S(1)} fusion(f32[40,64]{1,0:T(8,128)} %constant.215, f32[16]{0:T(128)} %param.21), kind=kLoop, calls=%fused_computation.51 | loop fusion | flops 245760 | bytes 174144 | tf_op jit(solution)/shard_map/div | solution.py:469
  5.6 1.1 slice.58
  6.7 0.2 rev.9
  6.9 1.4 %convolution_bitcast_fusion.1 = f32[32,31,128]{2,1,0:T(8,128)S(1)} fusion(f32[128,128,1]{1,0,2:T(8,128)} %constant.219, f32[32,31,128]{2,1,0:T(8,128)S(1)} %rev.9), kind=kOutput, calls=%fused_computation.9 | convolution fusion | flops 195035136 | bytes 1081344 | tf_op jit(solution)/shard_map/rab,bc->rac/dot_general | solution.py:478
  8.3 0.8 pad_add_fusion
  9.2 0.6 convolution_bitcast_fusion
  10.3 1.8 %fusion.16.own_ref = f32[16,40,128]{2,1,0:T(8,128)} fusion(f32[40,256,1]{1,0,2:T(8,128)S(1)} %copy-done.13, f32[16,128,64]{1,2,0:T(8,128)S(1)} %get-tuple-element.13, f32[16,128,64]{1,2,0:T(8,128)S(1)} %get-tuple-element.12, f32[16,128,128]{1,2,0:T(8,128)S(1)} %convolution_bitcast_fusion, f32[16,40,64]{2,1,0:T(8,128)S(1)} %fusion.24, f32[40]{0:T(128)S(1)} %copy-done.15, ...), kind=kOutput, calls=%fused_computation.13 | convolution fusion | flops 127287296 | bytes 2646216 | tf_op jit(solution)/shard_map/ry,pyg->prg/dot_general | solution.py:455
  12.0 1.0 fusion.60
  13.0 1.3 %copy.90 = f32[32,31,1]{1,0,2:T(8,128)S(1)} copy(f32[32,31,1]{2,1,0:T(8,128)} %get-tuple-element.8) | data formatting | bytes 7936
  14.4 0.3 copy.91
  15.0 0.2 slice_negate_fusion.1
  15.2 0.4 pad_maximum_fusion
  15.7 33.7 %ring_gather.1 = f32[16,16,40,128]{3,2,1,0:T(8,128)} custom-call(f32[16,40,128]{2,1,0:T(8,128)} %fusion.16.own_ref), custom_call_target="tpu_custom_call" | custom-call | tf_op jit(solution)/shard_map/ring_gather/pallas_call | solution.py:302
  49.4 1.3 %slice.74 = f32[256,1,128]{2,1,0:T(1,128)S(1)} slice(f32[256,40,128]{2,1,0:T(8,128)} %bitcast.54), slice={[0:256], [34:35], [0:128]} | slice | bytes 262144 | tf_op jit(solution)/shard_map/slice | solution.py:638
  51.3 0.5 select_reduce_fusion.1
  51.9 0.6 select_reduce_fusion.2
  52.7 2.5 %copy-done.1 = f32[16,16,40,128]{3,2,1,0:T(8,128)S(1)} copy-done((f32[16,16,40,128]{3,2,1,0:T(8,128)S(1)}, f32[16,16,40,128]{3,2,1,0:T(8,128)}, u32[]{:S(2)}) %copy-start.1) | copy-done | bytes 5242904
  55.2 12.2 %score_items.1 = f32[128,128]{1,0:T(8,128)S(1)} custom-call(s32[128]{0:T(128)S(1)} %reshape.226.pidx, s32[128]{0:T(128)S(1)} %reshape.227.ridx, f32[256,40,128]{2,1,0:T(8,128)S(1)} %bitcast.56, f32[32,40,128]{2,1,0:T(8,128)S(1)} %get-tuple-element.21.a_ref, f32[32,40,128]{2,1,0:T(8,128)S(1)} %get-tuple-element.22.b_ref, bf16[128,256]{1,0:T(8,128)(2,1)S(1)} %copy-done.4, ...), custom_call_target="tpu_custom_call" | custom-call | tf_op jit(solution)/shard_map/score_items/pallas_call | solution.py:424
  67.5 0.6 broadcast_in_dim.101.own_ref
  68.1 8.6 %share_scores.1 = f32[16,8,128]{2,1,0:T(8,128)} custom-call(f32[8,128]{1,0:T(8,128)} %broadcast_in_dim.101.own_ref), custom_call_target="tpu_custom_call" | custom-call | tf_op jit(solution)/shard_map/share_scores/pallas_call | solution.py:345
  76.7 0.8 slice.64
  77.8 0.4 select_reduce_fusion
  78.5 0.7 constant_dynamic-slice_fusion
  79.2 0.9 add_select_fusion.1
  80.4 0.5 fusion.19
  80.9 32.5 %build_volume.1 = f32[4,2,4,64,128]{4,3,2,1,0:T(8,128)S(1)} custom-call(s32[8,1024]{1,0:T(8,128)S(1)} %fusion.49.cidx_ref, f32[4,256]{1,0:T(4,128)S(1)} %fusion.73.post_ref, f32[10240,128]{1,0:T(8,128)} %bitcast.55, bf16[128,128]{1,0:T(8,128)(2,1)S(1)} %copy-done.5), custom_call_target="tpu_custom_call" | custom-call | tf_op jit(solution)/shard_map/build_volume/pallas_call | solution.py:593
  113.4 0.8 copy.88
  114.2 2.2 %reshape.230 = f32[4,128,2,256]{3,2,1,0:T(2,128)} reshape(f32[4,16,8,2,2,128]{5,4,3,2,1,0:T(2,128)S(1)} %copy.88) | data formatting | bytes 2097152 | tf_op jit(solution)/shard_map/reshape | solution.py:673
  (72 shorter events, 2.9 us)
Async XLA Ops:
  0.6 8.5 %copy-start = (f32[16,128,128]{2,1,0:T(8,128)S(1)}, f32[16,128,128]{2,1,0:T(8,128)}, u32[]{:S(2)}) copy-start(f32[16,128,128]{2,1,0:T(8,128)} %param.20) | copy-start | bytes 3145732
  0.6 7.6 %copy-start.7 = (f32[32,64,128]{2,1,0:T(8,128)S(1)}, f32[32,64,128]{2,1,0:T(8,128)}, u32[]{:S(2)}) copy-start(f32[32,64,128]{2,1,0:T(8,128)} %param.22) | copy-start | bytes 3145732
  6.7 2.5 %copy-start.8 = (f32[128,128,1]{0,1,2:T(8,128)S(1)}, f32[128,128,1]{0,1,2:T(8,128)}, u32[]{:S(2)}) copy-start(f32[128,128,1]{0,1,2:T(8,128)} %constant.217) | copy-start | bytes 196612
  8.3 1.5 %copy-start.9 = (f32[128,128]{1,0:T(8,128)S(1)}, f32[128,128]{1,0:T(8,128)}, u32[]{:S(2)}) copy-start(f32[128,128]{1,0:T(8,128)} %constant.212) | copy-start | bytes 196612
  8.3 1.6 %copy-start.10 = (f32[128,128]{1,0:T(8,128)S(1)}, f32[128,128]{1,0:T(8,128)}, u32[]{:S(2)}) copy-start(f32[128,128]{1,0:T(8,128)} %constant.213) | copy-start | bytes 196612
  9.2 1.1 copy-start.13
  9.2 1.1 copy-start.14
  9.2 1.1 copy-start.15
  15.7 35.6 %copy-start.12 = (s32[64]{0:T(128)S(1)}, s32[64]{0:T(128)}, u32[]{:S(2)}) copy-start(s32[64]{0:T(128)} %and_select_fusion) | copy-start | bytes 772
  15.7 35.7 %copy-start.11 = (pred[64,64]{1,0:T(32,128)(4,1)S(1)}, pred[64,64]{1,0:T(32,128)(4,1)}, u32[]{:S(2)}) copy-start(pred[64,64]{1,0:T(32,128)(4,1)} %constant.216) | copy-start | bytes 12292
  15.7 37.0 %copy-start.2 = (bf16[128,240]{1,0:T(8,128)(2,1)S(1)}, bf16[128,240]{1,0:T(8,128)(2,1)}, u32[]{:S(2)}) copy-start(bf16[128,240]{1,0:T(8,128)(2,1)} %constant.197.clone.cc_ref) | copy-start | bytes 184324
  15.7 37.0 %copy-start.3 = (bf16[128,256]{1,0:T(8,128)(2,1)S(1)}, bf16[128,256]{1,0:T(8,128)(2,1)}, u32[]{:S(2)}) copy-start(bf16[128,256]{1,0:T(8,128)(2,1)} %constant.196.clone.wlo_ref) | copy-start | bytes 196612
  15.7 37.0 %copy-start.4 = (bf16[128,256]{1,0:T(8,128)(2,1)S(1)}, bf16[128,256]{1,0:T(8,128)(2,1)}, u32[]{:S(2)}) copy-start(bf16[128,256]{1,0:T(8,128)(2,1)} %constant.195.clone.whi_ref) | copy-start | bytes 196612
  15.7 37.0 %copy-start.6 = (f32[8,128]{1,0:T(8,128)S(1)}, f32[8,128]{1,0:T(8,128)}, u32[]{:S(2)}) copy-start(f32[8,128]{1,0:T(8,128)} %constant.198.clone.pat_ref) | copy-start | bytes 12292
  52.7 2.5 %copy-start.1 = (f32[16,16,40,128]{3,2,1,0:T(8,128)S(1)}, f32[16,16,40,128]{3,2,1,0:T(8,128)}, u32[]{:S(2)}) copy-start(f32[16,16,40,128]{3,2,1,0:T(8,128)} %ring_gather.1) | copy-start | bytes 15728644
  67.4 13.5 %copy-start.5 = (bf16[128,128]{1,0:T(8,128)(2,1)S(1)}, bf16[128,128]{1,0:T(8,128)(2,1)}, u32[]{:S(2)}) copy-start(bf16[128,128]{1,0:T(8,128)(2,1)} %constant.199.clone.turn_ref) | copy-start | bytes 98308

commit v3 on v2

--- a/solution.py
+++ b/solution.py
@@ -302,8 +302,8 @@
     return pl.pallas_call(
         functools.partial(gather_kernel, chips),
         out_shape=jax.ShapeDtypeStruct((owner_count,) + payload.shape, payload.dtype),
-        in_specs=[pl.BlockSpec(memory_space=pl.ANY)],
-        out_specs=pl.BlockSpec(memory_space=pl.ANY),
+        in_specs=[pl.BlockSpec(memory_space=pltpu.VMEM)],
+        out_specs=pl.BlockSpec(memory_space=pltpu.VMEM),
         scratch_shapes=[
             pltpu.SemaphoreType.DMA,
             pltpu.SemaphoreType.DMA((2, depth, 2)),
@@ -311,62 +311,21 @@
             pltpu.SemaphoreType.DMA((chips, 2)),
             pltpu.SemaphoreType.DMA((chips, 2)),
         ],
-        compiler_params=pltpu.CompilerParams(collective_id=1, has_side_effects=True),
+        compiler_params=pltpu.CompilerParams(collective_id=1, has_side_effects=True, vmem_limit_bytes=24 << 20),
         name="ring_gather",
     )(payload)
 
 
-def share_kernel(count, own_ref, out_ref, local_sem, send_sem, recv_sem):
-    me = lax.axis_index("slab")
-    barrier = pltpu.get_barrier_semaphore()
-    others = [(me + step) % count for step in range(1, count)]
-    for other in others:
-        pl.semaphore_signal(barrier, inc=1, device_id={"slab": other}, device_id_type=MESH)
-    local = pltpu.make_async_copy(own_ref, out_ref.at[me], local_sem)
-    local.start()
-    pl.semaphore_wait(barrier, count - 1)
-    copies = []
-    for n, other in enumerate(others):
-        copy = pltpu.make_async_remote_copy(
-            src_ref=own_ref, dst_ref=out_ref.at[me], send_sem=send_sem.at[n],
-            recv_sem=recv_sem.at[n], device_id={"slab": other}, device_id_type=MESH)
-        copy.start()
-        copies.append(copy)
-    for n, copy in enumerate(copies):
-        copy.wait_send()
-        source = (me + count - 1 - n) % count
-        pltpu.make_async_remote_copy(
-            src_ref=own_ref, dst_ref=out_ref.at[source], send_sem=send_sem.at[n],
-            recv_sem=recv_sem.at[n], device_id={"slab": source}, device_id_type=MESH).wait_recv()
-    local.wait()
-
-
-def share(row, count):
-    return pl.pallas_call(
-        functools.partial(share_kernel, count),
-        out_shape=jax.ShapeDtypeStruct((count,) + row.shape, row.dtype),
-        in_specs=[pl.BlockSpec(memory_space=pltpu.VMEM)],
-        out_specs=pl.BlockSpec(memory_space=pltpu.VMEM),
-        scratch_shapes=[
-            pltpu.SemaphoreType.DMA,
-            pltpu.SemaphoreType.DMA((count - 1,)),
-            pltpu.SemaphoreType.DMA((count - 1,)),
-        ],
-        compiler_params=pltpu.CompilerParams(collective_id=2, has_side_effects=True),
-        name="share_scores",
-    )(row)
-
-
 GROUP = 8
 
 
-def score_kernel(pidx, ridx, half_ref, a_ref, b_ref, whi_ref, wlo_ref, cc_ref, pat_ref, out_ref):
+def score_kernel(pidx, ridx, spectra_ref, a_ref, b_ref, whi_ref, wlo_ref, cc_ref, pat_ref, slot_ref, out_ref):
     step = pl.program_id(0)
-    lines = half_ref.shape[1]
+    lines = a_ref.shape[1]
     f32, bf16 = jnp.float32, jnp.bfloat16
     products = []
     for e in range(GROUP):
-        spec = half_ref[pidx[step * GROUP + e]]
+        spec = spectra_ref[pidx[step * GROUP + e]]
         ref = ridx[step * GROUP + e]
         products.append(a_ref[ref] * spec + b_ref[ref] * pltpu.roll(spec, 64, 1))
     product = jnp.concatenate(products, axis=0)
@@ -391,7 +350,14 @@
         best = jnp.max(shifts, axis=0, keepdims=True)
         peaks += [best[:, :128], best[:, 128:]]
     peak = jnp.max(jnp.concatenate(peaks, axis=0), axis=1, keepdims=True)
-    out_ref[...] = jnp.broadcast_to(peak, (GROUP, 128))
+    value = peak * peak + EPSILON
+    slot = lax.broadcasted_iota(jnp.int32, out_ref.shape, 0) + step * GROUP
+
+    @pl.when(step == 0)
+    def _():
+        out_ref[...] = jnp.zeros_like(out_ref)
+
+    out_ref[...] += jnp.where(slot_ref[...] == slot, value, 0.0)
 
 
 def score_tables(image_side, frequency_total, lines):
@@ -415,19 +381,18 @@
     return whi, wlo, np.concatenate([chi, chi, clo], axis=1), pat
 
 
-def score_items(pidx, ridx, spectra, ref_a, ref_b, image_side, frequency_total):
-    slots = pidx.shape[0]
+def score_items(pidx, ridx, spectra, ref_a, ref_b, slots, image_side, frequency_total):
     lines = spectra.shape[1]
     whi, wlo, cc, pat = (jnp.asarray(t) for t in score_tables(image_side, frequency_total, lines))
     full = lambda arr: pl.BlockSpec(arr.shape, lambda i, *_: (0,) * arr.ndim, pipeline_mode=pl.Buffered(1))
-    args = (spectra, ref_a, ref_b, whi, wlo, cc, pat)
+    args = (spectra, ref_a, ref_b, whi, wlo, cc, pat, slots)
     return pl.pallas_call(
         score_kernel,
-        out_shape=jax.ShapeDtypeStruct((slots, 128), jnp.float32),
+        out_shape=jax.ShapeDtypeStruct((GROUP, slots.shape[1]), jnp.float32),
         grid_spec=pltpu.PrefetchScalarGridSpec(
-            num_scalar_prefetch=2, grid=(slots // GROUP,),
+            num_scalar_prefetch=2, grid=(pidx.shape[0] // GROUP,),
             in_specs=[full(arr) for arr in args],
-            out_specs=pl.BlockSpec((GROUP, 128), lambda i, *_: (i, 0))),
+            out_specs=pl.BlockSpec((GROUP, slots.shape[1]), lambda i, *_: (0, 0))),
         compiler_params=pltpu.CompilerParams(vmem_limit_bytes=40 << 20),
         name="score_items",
     )(pidx, ridx, *args)
@@ -488,35 +453,60 @@
     return jnp.concatenate([re, re], axis=2), jnp.concatenate([-im, im], axis=2)
 
 
-def volume_kernel(cidx_ref, post_ref, flat_ref, turn_ref, out_ref,
-                  s_hi, s_lo, m_hi, m_lo, edge, away, inbox, send_sem, recv_sem):
+def finish_kernel(count, tally_ref, cidx_ref, flat_ref, turn_ref, out_ref, post_ref,
+                  dense, everyone, s_hi, s_lo, m_hi, m_lo, edge, away, inbox,
+                  share_send, share_recv, send_sem, recv_sem):
     f32, bf16 = jnp.float32, jnp.bfloat16
     picks, n = post_ref.shape
     lines = flat_ref.shape[0] // n
     bands, halves = m_hi.shape[1], m_hi.shape[1] // 2
+    me = lax.axis_index("slab")
     peer = 1 - lax.axis_index("dp")
+    others = [(me + step) % count for step in range(1, count)]
     barrier = pltpu.get_barrier_semaphore()
     pl.semaphore_signal(barrier, inc=1, device_id={"dp": peer}, device_id_type=MESH)
-
+    for other in others:
+        pl.semaphore_signal(barrier, inc=1, device_id={"slab": other}, device_id_type=MESH)
+    dense[...] = jnp.sum(tally_ref[...], axis=0, keepdims=True)
     def split(value):
         high = value.astype(bf16)
         return high, (value - high.astype(f32)).astype(bf16)
 
-    for row in range(s_hi.shape[0]):
-        s_hi[row], s_lo[row] = split(flat_ref[pl.ds(row, n, stride=lines), :])
-
-    def build(j, carry):
-        where = cidx_ref[pl.ds(j, 1), :]
-        for part in range(2):
+    def prepare(first, stop):
+        for row in range(first, stop):
+            s_hi[row], s_lo[row] = split(flat_ref[pl.ds(row, n, stride=lines), :])
+
+    prepare(0, s_hi.shape[0] // 2)
+    pl.semaphore_wait(barrier, count)
+    shares = []
+    for i, other in enumerate(others):
+        copy = pltpu.make_async_remote_copy(
+            src_ref=dense, dst_ref=everyone.at[i], send_sem=share_send.at[i],
+            recv_sem=share_recv.at[i], device_id={"slab": other}, device_id_type=MESH)
+        copy.start()
+        shares.append(copy)
+    prepare(s_hi.shape[0] // 2, s_hi.shape[0])
+
+    scores = dense[...]
+    for i, copy in enumerate(shares):
+        copy.wait_recv()
+        scores = scores + everyone[i]
+    scores = [scores[:, k * n:(k + 1) * n] for k in range(picks)]
+    total = sum(scores[1:], scores[0])
+    for k in range(picks):
+        post_ref[k:k + 1, :] = scores[k] / total
+
+    def build(part):
+        def one(j, carry):
+            where = cidx_ref[pl.ds(j, 1), :]
             cell = lax.broadcasted_iota(jnp.int32, (n, n), 0) + part * n
-            total = jnp.zeros((n, n), f32)
+            value = jnp.zeros((n, n), f32)
             for k in range(picks):
-                total = total + jnp.where(where[:, k * n:(k + 1) * n] == cell, post_ref[k:k + 1, :], 0.0)
-            m_hi[part, j], m_lo[part, j] = split(total)
-        return carry
-
-    lax.fori_loop(0, bands, build, 0)
-    pl.semaphore_wait(barrier, 1)
+                value = value + jnp.where(where[:, k * n:(k + 1) * n] == cell, post_ref[k:k + 1, :], 0.0)
+            m_hi[part, j], m_lo[part, j] = split(value)
+            return carry
+
+        lax.fori_loop(0, bands, one, 0)
 
     def dot(x, y):
         return jnp.dot(x, y, preferred_element_type=f32)
@@ -524,7 +514,7 @@
     def product(part, j, hi, lo):
         return dot(m_hi[part, j], hi) + dot(m_lo[part, j], hi) + dot(m_hi[part, j], lo)
 
-    last = s_hi.shape[0] - 1
+    last = s_hi.shape[0]
     lane = lax.broadcasted_iota(jnp.int32, (n, 128), 1)
 
     def edges(part):
@@ -568,11 +558,13 @@
             device_id={"dp": peer}, device_id_type=MESH)
 
     pieces = away.shape[0]
+    build(0)
     edges(0)
     for ip in range(pieces):
         for u, p, value in chunk(0, ip):
             away[ip, u, p] = value
         copy_of(ip).start()
+    build(1)
     edges(1)
     for ip in range(pieces):
         for u, p, value in chunk(1, ip):
@@ -580,36 +572,45 @@
     for ip in range(pieces):
         copy_of(ip).wait_recv()
         out_ref[ip] = out_ref[ip] + inbox[ip]
+    for copy in shares:
+        copy.wait_send()
     for ip in range(pieces):
         copy_of(ip).wait_send()
 
 
-def build_volume(cidx, post, flat, half):
-    bands, n = cidx.shape[0], post.shape[1]
+def finish(tally, cidx, flat, count, lines, frequency_total):
+    bands, half = cidx.shape[0], frequency_total // 2
     lanes = flat.shape[1]
-    turn = jnp.asarray(mirror_matrix(lanes // 2), jnp.bfloat16)
+    n = flat.shape[0] // lines
+    items = cidx.shape[1]
+    turn = jnp.asarray(mirror_matrix(frequency_total), jnp.bfloat16)
     piece = (4, 2, 4, n // 4, lanes)
     vmem = pl.BlockSpec(memory_space=pltpu.VMEM)
     return pl.pallas_call(
-        volume_kernel,
-        out_shape=jax.ShapeDtypeStruct(piece, jnp.float32),
+        functools.partial(finish_kernel, count),
+        out_shape=(jax.ShapeDtypeStruct(piece, jnp.float32),
+                   jax.ShapeDtypeStruct((items // n, n), jnp.float32)),
         in_specs=[vmem] * 4,
-        out_specs=vmem,
+        out_specs=(vmem, vmem),
         scratch_shapes=[
-            pltpu.VMEM((half + 2, n, lanes), jnp.bfloat16),
-            pltpu.VMEM((half + 2, n, lanes), jnp.bfloat16),
+            pltpu.VMEM((1, items), jnp.float32),
+            pltpu.VMEM((count - 1, 1, items), jnp.float32),
+            pltpu.VMEM((half + 1, n, lanes), jnp.bfloat16),
+            pltpu.VMEM((half + 1, n, lanes), jnp.bfloat16),
             pltpu.VMEM((2, bands, n, n), jnp.bfloat16),
             pltpu.VMEM((2, bands, n, n), jnp.bfloat16),
             pltpu.VMEM((n, lanes), jnp.float32),
             pltpu.VMEM(piece, jnp.float32),
             pltpu.VMEM(piece, jnp.float32),
+            pltpu.SemaphoreType.DMA((count - 1,)),
+            pltpu.SemaphoreType.DMA((count - 1,)),
             pltpu.SemaphoreType.DMA((4,)),
             pltpu.SemaphoreType.DMA((4,)),
         ],
         compiler_params=pltpu.CompilerParams(
             collective_id=3, has_side_effects=True, vmem_limit_bytes=48 << 20),
-        name="build_volume",
-    )(cidx, post, flat, turn)
+        name="share_and_insert",
+    )(tally, cidx, flat, turn)
 
 
 def gather_device(images, defocus, references, orient_owner, orient_local, block_owner, block_cell):
@@ -647,15 +648,8 @@
     particle = (jnp.arange(count)[:, None] * parts + jnp.arange(items)[None, :] // picks)
     pick = lambda value: jnp.sum(jnp.where(mine, value[:, :, None], 0), axis=1).reshape(-1)
     pidx, ridx = pick(particle), pick(by_source % refs)
-    peaks = score_items(pidx, ridx, flat, ref_a, ref_b, side, frequency_total)[:, 0]
-    slot_scores = peaks * peaks + EPSILON
-    everyone = share(jnp.broadcast_to(slot_scores[None], (8, count * cap)), count)[:, 0]
-    table = everyone.reshape(count, count, cap).transpose(1, 0, 2).reshape(count, count * cap)
-    where = owner * cap + rank
-    scores = jnp.sum(
-        jnp.where(where[:, :, None] == jnp.arange(count * cap)[None, None, :], table[:, None, :], 0.0), axis=2)
-    scores = scores.reshape(count * parts, picks)
-    posterior = scores / jnp.sum(scores, axis=1, keepdims=True)
+    slots = jnp.where(owner == me, jnp.arange(count)[:, None] * cap + rank, -1)
+    slots = slots.reshape(count * parts, picks).T.reshape(1, -1)
     n = count * parts
     row_blocks, col_blocks = VY // band_rows, VX // frequency_total
     span = row_blocks // 2
@@ -668,10 +662,11 @@
     digits = jnp.concatenate([order // 32, order % 32], axis=0).astype(jnp.bfloat16)
     digits = jnp.dot(digits, named, preferred_element_type=jnp.float32).astype(jnp.int32)
     cidx = digits[:bands] * 32 + digits[bands:] - 1
-    built = build_volume(cidx, posterior.T, flat.reshape(n * lines, 2 * frequency_total), half)
+    tally = score_items(pidx, ridx, flat, ref_a, ref_b, slots, side, frequency_total)
+    built, weights = finish(tally, cidx, flat.reshape(n * lines, 2 * frequency_total), count, lines, frequency_total)
     built = built.reshape(band_rows, 2, 2, ZDEV, span, 2 * frequency_total)
     volume = built.transpose(3, 4, 0, 1, 2, 5).reshape(ZDEV, span * band_rows, 2, col_blocks * frequency_total)
-    own_posterior = lax.dynamic_slice_in_dim(posterior, me * parts, parts, axis=0)
+    own_posterior = lax.dynamic_slice_in_dim(weights, me * parts, parts, axis=1).T
     return (own_posterior, volume)
 
 

time: 117 us -> 113 us (0.966)
  Pallas kernels: 87 us -> 82.9 us
    unnamed x35 -> x40, local copies, waits for them, and re-layouts: 4.2 us -> 7.57 us
    pallas_call x3 -> x2, Pallas kernels: 53.3 us -> 50.1 us  [the longest x1 37.7 us: finish(): pl.pallas_call(functools.partial(finish_kernel, count), out_shape=(jax.Sh...]
    slice x1, local copies, waits for them, and re-layouts: 1.34 us -> 0.11 us  [gather_device(): meta = flat[:, meta_row]]
where the time goes in v3:
time: 113 us; the launch traced here: 112 us
  Pallas kernels  82.9 us (73%)
  local copies, waits for them, and re-layouts  15.2 us (13%)
  other arithmetic  9.36 us (8%)
  matrix products  3.75 us (3%)
    pallas_call x1, Pallas kernels, finish(): pl.pallas_call(functools.partial(finish_kernel, count), out_shape=(jax.Sh...  37.7 us
    pallas_call x1, Pallas kernels, ring_gather(): pl.pallas_call(functools.partial(gather_kernel, chips), out_shape=jax.Sha...  32.8 us
    pallas_call x1, Pallas kernels, score_items(): pl.pallas_call(score_kernel, out_shape=jax.ShapeDtypeStruct((GROUP, slots...  12.4 us
    unnamed x40, local copies, waits for them, and re-layouts  7.57 us

profile of v3, /device:TPU:0, one launch (start us, length us, event | category | flops | bytes accessed | tf_op | source)
XLA Modules:
  0.0 112.3 jit_solution(7340768535783678038)
XLA Ops:
  0.7 0.5 iota_compare_fusion.8
  1.3 0.6 iota_multiply_fusion.1
  1.8 0.5 and_select_fusion
  2.3 0.7 add_convert_fusion
  3.0 0.7 fusion.56
  4.2 2.0 %fusion.24 = f32[16,40,64]{2,1,0:T(8,128)S(1)} fusion(f32[40,64]{1,0:T(8,128)} %constant.213, f32[16]{0:T(128)} %param.21), kind=kLoop, calls=%fused_computation.49 | loop fusion | flops 245760 | bytes 174144 | tf_op jit(solution)/shard_map/div | solution.py:434
  6.2 1.1 slice.52
  7.3 0.2 rev.9
  7.5 1.4 %convolution_bitcast_fusion.1 = f32[32,31,128]{2,1,0:T(8,128)S(1)} fusion(f32[128,128,1]{1,0,2:T(8,128)} %constant.217, f32[32,31,128]{2,1,0:T(8,128)S(1)} %rev.9), kind=kOutput, calls=%fused_computation.9 | convolution fusion | flops 195035136 | bytes 1081344 | tf_op jit(solution)/shard_map/rab,bc->rac/dot_general | solution.py:443
  9.0 0.8 pad_add_fusion
  9.8 0.6 convolution_bitcast_fusion
  10.5 0.1 fusion.64
  10.6 0.2 convolution_add_fusion
  10.7 0.1 fusion.63
  10.9 1.0 fusion.16.own_ref
  12.0 1.2 %fusion.61 = (f32[32,31,1]{2,1,0:T(8,128)}, f32[32,31,1]{2,1,0:T(8,128)}) fusion(f32[32,64,128]{2,1,0:T(8,128)S(1)} %copy-done.8), kind=kLoop, calls=%fused_computation.125 | loop fusion | bytes 15872 | tf_op jit(solution)/shard_map/slice | solution.py:448
  13.1 1.3 %copy.79 = f32[32,31,1]{1,0,2:T(8,128)S(1)} copy(f32[32,31,1]{2,1,0:T(8,128)} %get-tuple-element.12) | data formatting | bytes 7936
  14.5 1.3 %copy.80 = f32[32,31,1]{1,0,2:T(8,128)S(1)} copy(f32[32,31,1]{2,1,0:T(8,128)} %get-tuple-element.13) | data formatting | bytes 7936
  16.1 0.2 slice_negate_fusion.1
  16.4 0.4 pad_maximum_fusion
  16.8 32.8 %ring_gather.1 = f32[16,16,40,128]{3,2,1,0:T(8,128)S(1)} custom-call(f32[16,40,128]{2,1,0:T(8,128)S(1)} %fusion.16.own_ref), custom_call_target="tpu_custom_call" | custom-call | tf_op jit(solution)/shard_map/ring_gather/pallas_call | solution.py:302
  49.7 2.3 %copy-done.1 = f32[16,16,40,128]{3,2,1,0:T(8,128)} copy-done((f32[16,16,40,128]{3,2,1,0:T(8,128)}, f32[16,16,40,128]{3,2,1,0:T(8,128)S(1)}, u32[]{:S(2)}) %copy-start.1) | copy-done | bytes 5242904
  52.3 0.9 add_select_fusion.1
  53.9 0.5 select_reduce_fusion
  54.4 0.6 select_reduce_fusion.1
  55.2 0.5 fusion.19
  56.0 2.5 %copy-done.2 = f32[16,16,40,128]{3,2,1,0:T(8,128)S(1)} copy-done((f32[16,16,40,128]{3,2,1,0:T(8,128)S(1)}, f32[16,16,40,128]{3,2,1,0:T(8,128)}, u32[]{:S(2)}) %copy-start.2) | copy-done | bytes 5242904
  58.5 12.4 %score_items.1.tally_ref = f32[8,1024]{1,0:T(8,128)S(1)} custom-call(s32[128]{0:T(128)S(1)} %reshape.210.pidx, s32[128]{0:T(128)S(1)} %reshape.211.ridx, f32[256,40,128]{2,1,0:T(8,128)S(1)} %bitcast.57, f32[32,40,128]{2,1,0:T(8,128)S(1)} %get-tuple-element.25.a_ref, f32[32,40,128]{2,1,0:T(8,128)S(1)} %get-tuple-element.26.b_ref, ...), custom_call_target="tpu_custom_call" | custom-call | tf_op jit(solution)/shard_map/score_items/pallas_call | solution.py:389
  70.9 37.7 %share_and_insert.1 = (f32[4,2,4,64,128]{4,3,2,1,0:T(8,128)S(1)}, f32[4,256]{1,0:T(4,128)S(1)}) custom-call(f32[8,1024]{1,0:T(8,128)S(1)} %score_items.1.tally_ref, s32[8,1024]{1,0:T(8,128)S(1)} %fusion.50.cidx_ref, f32[10240,128]{1,0:T(8,128)} %bitcast.56, bf16[128,128]{1,0:T(8,128)(2,1)S(1)} %copy-done.6), custom_call_target="tpu_custom_call" | custom-call | tf_op jit(solution)/shard_map/share_and_insert/pallas_call | solution.py:589
  108.6 0.7 dynamic-slice_bitcast_fusion
  109.3 0.8 copy.77
  110.1 2.2 %reshape.214 = f32[4,128,2,256]{3,2,1,0:T(2,128)} reshape(f32[4,16,8,2,2,128]{5,4,3,2,1,0:T(2,128)S(1)} %copy.77) | data formatting | bytes 2097152 | tf_op jit(solution)/shard_map/reshape | solution.py:668
  (69 shorter events, 2.4 us)
Async XLA Ops:
  0.6 9.2 %copy-start = (f32[16,128,128]{2,1,0:T(8,128)S(1)}, f32[16,128,128]{2,1,0:T(8,128)}, u32[]{:S(2)}) copy-start(f32[16,128,128]{2,1,0:T(8,128)} %param.20) | copy-start | bytes 3145732
  0.6 8.3 %copy-start.8 = (f32[32,64,128]{2,1,0:T(8,128)S(1)}, f32[32,64,128]{2,1,0:T(8,128)}, u32[]{:S(2)}) copy-start(f32[32,64,128]{2,1,0:T(8,128)} %param.22) | copy-start | bytes 3145732
  7.3 2.5 %copy-start.9 = (f32[128,128,1]{0,1,2:T(8,128)S(1)}, f32[128,128,1]{0,1,2:T(8,128)}, u32[]{:S(2)}) copy-start(f32[128,128,1]{0,1,2:T(8,128)} %constant.215) | copy-start | bytes 196612
  8.9 1.5 %copy-start.10 = (f32[128,128]{1,0:T(8,128)S(1)}, f32[128,128]{1,0:T(8,128)}, u32[]{:S(2)}) copy-start(f32[128,128]{1,0:T(8,128)} %constant.210) | copy-start | bytes 196612
  8.9 1.7 %copy-start.11 = (f32[128,128]{1,0:T(8,128)S(1)}, f32[128,128]{1,0:T(8,128)}, u32[]{:S(2)}) copy-start(f32[128,128]{1,0:T(8,128)} %constant.211) | copy-start | bytes 196612
  9.8 1.1 copy-start.15
  9.8 1.1 copy-start.16
  9.8 1.1 copy-start.17
  49.6 4.2 %copy-start.13 = (s32[16]{0:T(128)S(1)}, s32[16]{0:T(128)}, u32[]{:S(2)}) copy-start(s32[16]{0:T(128)} %iota_multiply_fusion.1) | copy-start | bytes 196
  49.6 4.2 %copy-start.14 = (s32[64]{0:T(128)S(1)}, s32[64]{0:T(128)}, u32[]{:S(2)}) copy-start(s32[64]{0:T(128)} %and_select_fusion) | copy-start | bytes 772
  49.6 4.3 %copy-start.12 = (pred[64,64]{1,0:T(32,128)(4,1)S(1)}, pred[64,64]{1,0:T(32,128)(4,1)}, u32[]{:S(2)}) copy-start(pred[64,64]{1,0:T(32,128)(4,1)} %constant.214) | copy-start | bytes 12292
  49.7 2.3 %copy-start.1 = (f32[16,16,40,128]{3,2,1,0:T(8,128)}, f32[16,16,40,128]{3,2,1,0:T(8,128)S(1)}, u32[]{:S(2)}) copy-start(f32[16,16,40,128]{3,2,1,0:T(8,128)S(1)} %ring_gather.1) | copy-start | bytes 15728644
  52.3 3.7 %copy-start.3 = (bf16[128,240]{1,0:T(8,128)(2,1)S(1)}, bf16[128,240]{1,0:T(8,128)(2,1)}, u32[]{:S(2)}) copy-start(bf16[128,240]{1,0:T(8,128)(2,1)} %constant.195.clone.cc_ref) | copy-start | bytes 184324
  52.3 3.7 %copy-start.4 = (bf16[128,256]{1,0:T(8,128)(2,1)S(1)}, bf16[128,256]{1,0:T(8,128)(2,1)}, u32[]{:S(2)}) copy-start(bf16[128,256]{1,0:T(8,128)(2,1)} %constant.194.clone.wlo_ref) | copy-start | bytes 196612
  52.3 3.7 %copy-start.5 = (bf16[128,256]{1,0:T(8,128)(2,1)S(1)}, bf16[128,256]{1,0:T(8,128)(2,1)}, u32[]{:S(2)}) copy-start(bf16[128,256]{1,0:T(8,128)(2,1)} %constant.193.clone.whi_ref) | copy-start | bytes 196612
  52.3 3.7 %copy-start.7 = (f32[8,128]{1,0:T(8,128)S(1)}, f32[8,128]{1,0:T(8,128)}, u32[]{:S(2)}) copy-start(f32[8,128]{1,0:T(8,128)} %constant.196.clone.pat_ref) | copy-start | bytes 12292
  56.0 2.5 %copy-start.2 = (f32[16,16,40,128]{3,2,1,0:T(8,128)S(1)}, f32[16,16,40,128]{3,2,1,0:T(8,128)}, u32[]{:S(2)}) copy-start(f32[16,16,40,128]{3,2,1,0:T(8,128)} %copy-done.1) | copy-start | bytes 15728644
  58.5 12.4 %copy-start.6 = (bf16[128,128]{1,0:T(8,128)(2,1)S(1)}, bf16[128,128]{1,0:T(8,128)(2,1)}, u32[]{:S(2)}) copy-start(bf16[128,128]{1,0:T(8,128)(2,1)} %constant.197.clone.turn_ref) | copy-start | bytes 98308
